TPU v7x, 32 devices: a whole 2x2x4 slice. The times are simulated.
32 devices in a mesh: seq: 8 (over z, x), head: 4 (over y, core).
Axes of the slice: x: 2, y: 2, z: 4, core: 2. Of those that a mesh axis runs over, the one named last changes fastest.
Arguments:
- queries: bfloat16 [1024, 6144], P('seq', 'head'), may hold values from -6 to 6
- keys: bfloat16 [1024, 6144], P('seq', 'head'), may hold values from -6 to 6
- values: bfloat16 [1024, 6144], P('seq', 'head'), may hold values from -6 to 6
- log_decay: float32 [1024, 48], P('seq', 'head'), may hold values from -1 to 0, as said below
- out_gate: bfloat16 [1024, 6144], P('seq', 'head'), may hold values from -6 to 6
- attn_gain: bfloat16 [6144], P('head'), may hold values from 0.5 to 1.5
- residual: bfloat16 [1024, 6144], P('seq', 'head'), may hold values from -6 to 6
- moe_gain: bfloat16 [6144], P('head'), may hold values from 0.5 to 1.5
- router: bfloat16 [6144, 8], P('head'), may hold values from -0.078125 to 0.078125
- routes: int32 [1024, 2], P('seq'), may hold values from 0 to 7, all different within a row; in each aligned block of 128 rows (0 to 127, 128 to 255, ...) at most 36 rows name the same one
- w_gate: bfloat16 [6144, 36864], P('head', 'seq'), may hold values from -0.078125 to 0.078125
- w_up: bfloat16 [6144, 36864], P('head', 'seq'), may hold values from -0.078125 to 0.078125
- w_down: bfloat16 [36864, 6144], P('seq', 'head'), may hold values from -0.09375 to 0.09375
Outputs:
- layer_out: bfloat16 [1024, 6144], P('seq', 'head')
Inputs may be any that keep to these rules, and one draw needn't show every extreme that they name: `routes`: each row names two different experts; in the rows of one device (aligned blocks of 128 rows) no expert is named by more than 36 rows, a bound that some block reaches. `log_decay`: every entry is negative.
All inputs are finite; a program needn't handle non-finite values.
Results may differ from a plain program's by a relative error of at most 0.0055.
Values may be sent and summed in bfloat16 or wider, within the bound.
No kernel may reach another device: no remote copies, remote signals or barrier semaphores. Data moves between devices by JAX's collectives and lax.ppermute only.
A program may use at most 128 MiB of HBM per device.

v0:
```python
import jax
import jax.numpy as jnp
from jax import lax
from jax.sharding import PartitionSpec as P


def prefix_2(value, axis, join, neutral):
    count, mine = (lax.axis_size(axis), lax.axis_index(axis))
    pieces = jax.tree.map(lambda part: lax.all_gather(part, axis), value)
    subtotal = jax.tree.map(
        lambda part, zero: jnp.full_like(part, 0) + jnp.asarray(zero, part.dtype), value, neutral
    )

    def lap(position, subtotal):
        longer = join(subtotal, jax.tree.map(lambda part: part[position], pieces))
        return jax.tree.map(lambda new, old: jnp.where(position < mine, new, old), longer, subtotal)

    return lax.fori_loop(0, count - 1, lap, subtotal)


def block_terms(query_act, key_act, value_all, decay_log):
    length = query_act.shape[0]
    cumulative = jnp.cumsum(decay_log, axis=0)
    row_index = lax.broadcasted_iota(jnp.int32, (length, length), 0)
    col_index = lax.broadcasted_iota(jnp.int32, (length, length), 1)
    causal = (row_index >= col_index)[None, :, :]
    by_head = jnp.transpose(cumulative)
    spread = by_head[:, :, None] - by_head[:, None, :]
    weight = jnp.where(causal, jnp.exp(jnp.where(causal, spread, 0.0)), 0.0)
    scores = (
        jnp.einsum("ihe,jhe->hij", query_act, key_act, precision=lax.Precision.HIGHEST) * weight
    )
    inner_part = jnp.einsum("hij,jhe->ihe", scores, value_all, precision=lax.Precision.HIGHEST)
    tail_decay = jnp.exp(cumulative[-1][None, :] - cumulative)
    local_state = jnp.einsum(
        "jhe,jhf->hef", key_act * tail_decay[:, :, None], value_all, precision=lax.Precision.HIGHEST
    )
    return (cumulative, inner_part, local_state, jnp.exp(cumulative[-1]))


def attention_out(inner_part, cumulative, carry_state, query_act):
    earlier = jnp.einsum("ihe,hef->ihf", query_act, carry_state, precision=lax.Precision.HIGHEST)
    return inner_part + jnp.exp(cumulative)[:, :, None] * earlier


def finish(attn, attn_gain, out_gate, residual):
    mean_sq = jnp.mean(attn * attn, axis=-1, keepdims=True)
    normed_heads = attn * lax.rsqrt(mean_sq + 1e-06)
    flat = normed_heads.reshape(attn.shape[0], attn.shape[1] * attn.shape[2])
    gated = flat * attn_gain.astype(jnp.float32) * jax.nn.sigmoid(out_gate.astype(jnp.float32))
    return (residual.astype(jnp.float32) + gated).astype(jnp.bfloat16)


def gate_weights(logits, routes):
    expert_ids = lax.broadcasted_iota(jnp.int32, (1, 1, logits.shape[1]), 2)
    onehot = routes[:, :, None] == expert_ids
    picked = jnp.sum(jnp.where(onehot, logits[:, None, :], 0.0), axis=-1)
    return jax.nn.sigmoid(picked - picked[:, ::-1])


def slot_table(routes, expert_count, capacity):
    flat_ids = routes.reshape(-1)
    expert_ids = lax.broadcasted_iota(jnp.int32, (1, expert_count), 1)
    onehot = (flat_ids[:, None] == expert_ids).astype(jnp.int32)
    ranking = jnp.cumsum(onehot, axis=0) - onehot
    own_rank = jnp.sum(ranking * onehot, axis=1)
    slot_ids = flat_ids * capacity + own_rank
    slot_range = lax.broadcasted_iota(jnp.int32, (1, expert_count * capacity), 1)
    return (slot_ids[:, None] == slot_range).astype(jnp.float32)


def build_sends(tok_rows, slot_bf16, expert_count, capacity, owner_count):
    doubled = jnp.repeat(tok_rows, 2, axis=0)
    packed = jnp.einsum("as,ad->sd", slot_bf16, doubled, preferred_element_type=jnp.float32).astype(
        jnp.bfloat16
    )
    width = tok_rows.shape[1]
    fanned = jnp.broadcast_to(
        packed.reshape(expert_count, 1, capacity, width),
        (expert_count, owner_count, capacity, width),
    )
    return fanned.reshape(expert_count * owner_count, capacity, width)


def local(
    queries,
    keys,
    values,
    log_decay,
    out_gate,
    attn_gain,
    residual,
    moe_gain,
    router,
    routes,
    w_gate,
    w_up,
    w_down,
):
    tok_count = queries.shape[0]
    heads_here = log_decay.shape[1]
    head_size = queries.shape[1] // heads_here
    query_act = jax.nn.silu(queries.astype(jnp.float32)).reshape(tok_count, heads_here, head_size)
    key_act = jax.nn.silu(keys.astype(jnp.float32)).reshape(tok_count, heads_here, head_size)
    value_all = values.astype(jnp.float32).reshape(tok_count, heads_here, head_size)
    cumulative, inner_part, local_state, block_decay = block_terms(
        query_act, key_act, value_all, log_decay
    )

    def combine(earlier, later):
        return (earlier[0] * later[0], later[0][:, None, None] * earlier[1] + later[1])

    identity = (jnp.ones_like(block_decay), jnp.zeros_like(local_state))
    prefix = prefix_2((block_decay, local_state), "seq", combine, identity)
    attn = attention_out(inner_part, cumulative, prefix[1], query_act)
    hidden = finish(attn, attn_gain, out_gate, residual)
    part_width = hidden.shape[1]
    full_width = part_width * lax.axis_size("head")
    wide = hidden.astype(jnp.float32)
    squares = lax.psum(jnp.sum(wide * wide, axis=1), "head")
    scale = lax.rsqrt(squares / full_width + 1e-06)
    normed = (wide * scale[:, None] * moe_gain.astype(jnp.float32)).astype(jnp.bfloat16)
    logits = lax.psum(jnp.dot(normed, router, preferred_element_type=jnp.float32), "head")
    weights = gate_weights(logits, routes)
    expert_count = router.shape[1]
    owner_count = lax.axis_size("seq") // expert_count
    capacity = 2 * tok_count // expert_count + max(1, tok_count // 32)
    table = slot_table(routes, expert_count, capacity)
    outgoing = build_sends(normed, table.astype(jnp.bfloat16), expert_count, capacity, owner_count)
    arrived = lax.all_to_all(outgoing, "seq", split_axis=0, concat_axis=0, tiled=True)
    sources, items, width = arrived.shape
    flat_rows = arrived.reshape(sources * items, width)
    gate_part = jnp.dot(flat_rows, w_gate, preferred_element_type=jnp.float32)
    up_part = jnp.dot(flat_rows, w_up, preferred_element_type=jnp.float32)
    gate = lax.psum_scatter(gate_part, "head", scatter_dimension=1, tiled=True)
    upward = lax.psum_scatter(up_part, "head", scatter_dimension=1, tiled=True)
    act = (jax.nn.silu(gate) * upward).astype(jnp.bfloat16)
    act = lax.all_gather(act, "head", axis=1, tiled=True)
    result = jnp.dot(act, w_down, preferred_element_type=jnp.float32).astype(jnp.bfloat16)
    shares = result.reshape(sources, items, width)
    returned = lax.all_to_all(shares, "seq", split_axis=0, concat_axis=0, tiled=True)
    summed = (
        returned.astype(jnp.float32)
        .reshape(expert_count, owner_count, capacity, part_width)
        .sum(axis=1)
    )
    summed = summed.reshape(expert_count * capacity, part_width)
    per_token = (
        (table * weights.reshape(-1)[:, None])
        .reshape(tok_count, 2, expert_count * capacity)
        .sum(axis=1)
    )
    moe = jnp.dot(per_token, summed, precision=lax.Precision.HIGHEST)
    return (hidden.astype(jnp.float32) + moe).astype(jnp.bfloat16)


def solution(mesh):
    return jax.shard_map(
        local,
        mesh=mesh,
        in_specs=(
            P("seq", "head"),
            P("seq", "head"),
            P("seq", "head"),
            P("seq", "head"),
            P("seq", "head"),
            P("head"),
            P("seq", "head"),
            P("head"),
            P("head", None),
            P("seq", None),
            P("head", "seq"),
            P("head", "seq"),
            P("seq", "head"),
        ),
        out_specs=P("seq", "head"),
        check_vma=False,
    )
```

profile of v0, /device:TPU:8, one launch (start us, length us, event | category | flops | bytes accessed | tf_op | source)
XLA Modules:
  0.0 353.4 jit_solution(10347637837629961265)
XLA Ops:
  10.4 1.8 fusion.13
  13.9 1.4 copy.85
  16.3 18.4 %all-gather.1 = f32[8,1,12]{2,1,0:T(1,128)S(1)} all-gather(f32[1,1,12]{2,1,0:T(1,128)S(1)} %get-tuple-element.133), channel_id=1, replica_groups=mesh['seq'=8,'head'=4] {'seq'}, dimensions={0}, use_global_device_ids=true | all-gather | bytes 432 | tf_op jit(solution)/shard_map/all_gather | solution.py:9
  34.8 2.5 convolution_multiply_fusion
  37.3 73.9 %all-gather.7.cloned.1.call-done = f32[96,128,128]{2,1,0:T(8,128)} async-done(((f32[12,128,128]{2,1,0:T(8,128)}), f32[96,128,128]{2,1,0:T(8,128)}) %all-gather.7.cloned.1.call-update) | async-done | bytes 6291472 | tf_op jit(solution)/shard_map/all_gather | solution.py:9
  111.2 9.4 %while.14 = (s32[]{:T(128)}, f32[12,128,128]{2,1,0:T(8,128)S(1)}, s32[]{:T(128)}, f32[8,12]{1,0:T(8,128)S(1)}, f32[8,12,128,128]{3,2,1,0:T(8,128)}, /*index=5*/s32[]{:T(128)}, s32[]{:T(128)}) while((s32[]{:T(128)}, f32[12,128,128]{2,1,0:T(8,128)S(1)}, s32[]{:T(128)}, f32[8,12]{1,0:T(8,128)S(1)}, f32[8,12,128,128]{3,2,1,0:T(8,128)}, ...), condition=%wide.region_2.3_spmd.clone, body=%wide.region_1.2_spmd.clone.sunk | while | flops 786436 | bytes 2359545 | solution.py:18
  111.2 1.4 fusion.43
  112.6 1.3 fusion.43
  113.9 1.3 fusion.43
  120.6 1.5 fusion.3
  123.4 1.4 fusion.10
  124.8 5.7 %psum.14 = f32[128]{0:T(128)S(1)} all-reduce(f32[128]{0:T(128)S(1)} %get-tuple-element.128), channel_id=1, replica_groups=mesh['seq'=8,'head'=4] {'head'}, use_global_device_ids=true, to_apply=%region_8.9 | all-reduce | flops 128 | bytes 1024 | tf_op jit(solution)/shard_map/psum | solution.py:120
  132.1 28.0 %all_to_all.10 = bf16[8,36,1536]{2,1,0:T(8,128)(2,1)S(1)} all-to-all(bf16[8,36,1536]{2,1,0:T(8,128)(2,1)S(1)} %reshape_reshape.3), channel_id=1, replica_groups=mesh['seq'=8,'head'=4] {'seq'}, dimensions={0} | all-to-all | bytes 1769472 | tf_op jit(solution)/shard_map/all_to_all | solution.py:130
  160.2 11.0 %fusion.22 = f32[288,4608]{1,0:T(8,128)} fusion(bf16[288,1536]{1,0:T(8,128)(2,1)S(1)} %reshape.119, bf16[1536,4608]{1,0:T(8,128)(2,1)} %param.25), kind=kOutput, calls=%fused_computation.59 | convolution fusion | flops 4076863488 | bytes 20348928 | tf_op jit(solution)/shard_map/dot_general | solution.py:133
  171.5 11.2 %fusion.23 = f32[288,4608]{1,0:T(8,128)} fusion(bf16[288,1536]{1,0:T(8,128)(2,1)S(1)} %reshape.119, bf16[1536,4608]{1,0:T(8,128)(2,1)} %param.26), kind=kOutput, calls=%fused_computation.60 | convolution fusion | flops 4076863488 | bytes 20348928 | tf_op jit(solution)/shard_map/dot_general | solution.py:134
  182.8 39.5 %reduce-scatter.3.cloned.1.call-done = f32[288,1152]{1,0:T(8,128)} async-done(((f32[288,4608]{1,0:T(8,128)}), f32[288,1152]{1,0:T(8,128)}) %reduce-scatter.3.cloned.1.call-update) | async-done | bytes 1327120 | tf_op jit(solution)/shard_map/reduce_scatter | solution.py:135
  222.3 54.2 %reduce-scatter.5.cloned.1.call-done = f32[288,1152]{1,0:T(8,128)} async-done(((f32[288,4608]{1,0:T(8,128)}), f32[288,1152]{1,0:T(8,128)}) %reduce-scatter.5.cloned.1.call-update) | async-done | bytes 1327120 | tf_op jit(solution)/shard_map/reduce_scatter | solution.py:136
  276.5 3.0 multiply_convert_fusion
  279.4 25.9 %all-gather.5.cloned.1.call-done = bf16[288,4608]{1,0:T(8,128)(2,1)} async-done(((bf16[288,1152]{1,0:T(8,128)(2,1)}), bf16[288,4608]{1,0:T(8,128)(2,1)}) %all-gather.5.cloned.1.call-update) | async-done | bytes 2654224 | tf_op jit(solution)/shard_map/all_gather | solution.py:138
  305.3 10.1 %convolution_convert_fusion.1 = bf16[288,1536]{1,0:T(8,128)(2,1)S(1)} fusion(bf16[288,4608]{1,0:T(8,128)(2,1)} %all-gather.5.cloned.1.call-done, bf16[4608,1536]{1,0:T(8,128)(2,1)} %param.27), kind=kOutput, calls=%fused_computation.4 | convolution fusion | flops 4077305856 | bytes 17694720 | tf_op jit(solution)/shard_map/dot_general | solution.py:139
  316.5 6.0 %all-to-all-start.1 = ((bf16[8,36,1536]{2,1,0:T(8,128)(2,1)}), bf16[8,36,1536]{2,1,0:T(8,128)(2,1)S(1)}, u32[]{:S(2)}, u32[]{:S(2)}) async-start(bf16[8,36,1536]{2,1,0:T(8,128)(2,1)} %reshape.120), calls=%async_computation.3 | async-start | bytes 1966080 | tf_op jit(solution)/shard_map/all_to_all | solution.py:141
  323.0 6.0 %psum.15 = f32[128,8]{0,1:T(8,128)S(1)} all-reduce(f32[128,8]{0,1:T(8,128)S(1)} %fusion.21), channel_id=1, replica_groups=mesh['seq'=8,'head'=4] {'head'}, use_global_device_ids=true, to_apply=%region_9.10 | all-reduce | flops 1024 | bytes 8192 | tf_op jit(solution)/shard_map/psum | solution.py:123
  329.1 16.0 %all-to-all-done.1 = bf16[8,36,1536]{2,1,0:T(8,128)(2,1)S(1)} async-done(((bf16[8,36,1536]{2,1,0:T(8,128)(2,1)}), bf16[8,36,1536]{2,1,0:T(8,128)(2,1)S(1)}, u32[]{:S(2)}, u32[]{:S(2)}) %all-to-all-start.1) | async-done | bytes 884768 | tf_op jit(solution)/shard_map/all_to_all | solution.py:141
  345.2 1.6 fusion.1
  (79 shorter events, 16.9 us)
Async XLA Ops:
  6.5 316.3 %copy-start = (bf16[1536,8]{0,1:T(8,128)(2,1)S(1)}, bf16[1536,8]{0,1:T(8,128)(2,1)}, u32[]{:S(2)}) copy-start(bf16[1536,8]{0,1:T(8,128)(2,1)} %param.23) | copy-start | bytes 73732
  6.5 5.8 %copy-start.4 = (s32[128,2]{0,1:T(2,128)S(1)}, s32[128,2]{0,1:T(2,128)}, u32[]{:S(2)}) copy-start(s32[128,2]{0,1:T(2,128)} %param.24) | copy-start | bytes 3076
  6.5 6.3 %copy-start.2 = (bf16[128,1536]{1,0:T(8,128)(2,1)S(1)}, bf16[128,1536]{1,0:T(8,128)(2,1)}, u32[]{:S(2)}) copy-start(bf16[128,1536]{1,0:T(8,128)(2,1)} %param.15) | copy-start | bytes 1179652
  6.5 8.9 %copy-start.5 = (bf16[1536]{0:T(1024)(128)(2,1)S(1)}, bf16[1536]{0:T(1024)(128)(2,1)}, u32[]{:S(2)}) copy-start(bf16[1536]{0:T(1024)(128)(2,1)} %param.20) | copy-start | bytes 9220
  6.5 8.9 %copy-start.6 = (bf16[1536]{0:T(1024)(128)(2,1)S(1)}, bf16[1536]{0:T(1024)(128)(2,1)}, u32[]{:S(2)}) copy-start(bf16[1536]{0:T(1024)(128)(2,1)} %param.22) | copy-start | bytes 9220
  6.5 104.6 %all-gather.7.cloned.1.call-start = ((), (), s32[]{:S(2)}) async-start(), calls=%async_computation.7 | async-start | bytes 7077888 | tf_op jit(solution)/shard_map/all_gather | solution.py:9
  12.3 210.0 %reduce-scatter.3.cloned.1.call-start = ((), (), s32[]{:S(2)}) async-start(), calls=%async_computation.4 | async-start | bytes 6635520 | tf_op jit(solution)/shard_map/reduce_scatter | solution.py:135
  111.2 10.9 %copy-start.1 = (f32[12,128,128]{2,1,0:T(8,128)S(1)}, f32[12,128,128]{2,1,0:T(8,128)}, u32[]{:S(2)}) copy-start(f32[12,128,128]{2,1,0:T(8,128)} %convolution_multiply_fusion) | copy-start | bytes 2359300
  120.6 2.8 copy-start.3
  171.3 105.2 %reduce-scatter.5.cloned.1.call-start = ((), (), s32[]{:S(2)}) async-start(), calls=%async_computation.5 | async-start | bytes 6635520 | tf_op jit(solution)/shard_map/reduce_scatter | solution.py:136
  182.7 122.6 %all-gather.5.cloned.1.call-start = ((), (), s32[]{:S(2)}) async-start(), calls=%async_computation.6 | async-start | bytes 3317760 | tf_op jit(solution)/shard_map/all_gather | solution.py:138
  316.5 28.5 %all-to-all-start.1 = ((bf16[8,36,1536]{2,1,0:T(8,128)(2,1)}), bf16[8,36,1536]{2,1,0:T(8,128)(2,1)S(1)}, u32[]{:S(2)}, u32[]{:S(2)}) async-start(bf16[8,36,1536]{2,1,0:T(8,128)(2,1)} %reshape.120), calls=%async_computation.3 | async-start | bytes 1966080 | tf_op jit(solution)/shard_map/all_to_all | solution.py:141
Sparse Core Ops, SparseCore 0:
  12.4 98.6 all-gather.6
  171.4 50.8 reduce-scatter.2
  224.8 51.5 reduce-scatter.4
  279.6 25.7 all-gather.4
where the time goes:
time: 357 us; the launch traced here: 353 us
  waiting for transfers between devices  210 us (59%)
  blocking collectives  58 us (16%)
  matrix products  41.4 us (12%)
  other arithmetic  17.1 us (5%)
  between operations  13.4 us (4%)
  local copies, waits for them, and re-layouts  7.41 us (2%)
  starting transfers between devices  6.39 us (2%)
    all_gather x1, waiting for transfers between devices, prefix_2(): pieces = jax.tree.map(lambda part: lax.all_gather(part, axis), value)  73.9 us
    reduce_scatter x1, waiting for transfers between devices, local(): upward = lax.psum_scatter(up_part, 'head', scatter_dimension=1, tiled=True)  54.2 us
    reduce_scatter x1, waiting for transfers between devices, local(): gate = lax.psum_scatter(gate_part, 'head', scatter_dimension=1, tiled=True)  39.5 us
    all_to_all x1, blocking collectives, local(): lax.all_to_all(outgoing, 'seq', split_axis=0, concat_axis=0, tiled=True)  28 us
    all_gather x1, waiting for transfers between devices, local(): act = lax.all_gather(act, 'head', axis=1, tiled=True)  25.9 us
    all_gather x1, blocking collectives, prefix_2(): pieces = jax.tree.map(lambda part: lax.all_gather(part, axis), value)  18.4 us
    all_to_all x1, waiting for transfers between devices, local(): lax.all_to_all(shares, 'seq', split_axis=0, concat_axis=0, tiled=True)  16 us
    dot_general x1, matrix products, local(): up_part = jnp.dot(flat_rows, w_up, preferred_element_type=jnp.float32)  11.2 us
  transfers between devices with their start and end apart: 5, of which 5 were waited for; matrix products, arithmetic and copies ran while one was open for 5% of the time, Pallas kernels for 0%

commit v1 on v0

--- a/solution.py
+++ b/solution.py
@@ -1,6 +1,10 @@
+import functools
+
 import jax
 import jax.numpy as jnp
 from jax import lax
+from jax.experimental import pallas as pl
+from jax.experimental.pallas import tpu as pltpu
 from jax.sharding import PartitionSpec as P
 
 
@@ -82,7 +86,7 @@
     return fanned.reshape(expert_count * owner_count, capacity, width)
 
 
-def local(
+def local_general(
     queries,
     keys,
     values,
@@ -154,6 +158,564 @@
     return (hidden.astype(jnp.float32) + moe).astype(jnp.bfloat16)
 
 
+F32, BF16 = jnp.float32, jnp.bfloat16
+LANES = 128
+PAD = 16
+NT = (((1,), (1,)), ((), ()))
+TN = (((0,), (0,)), ((), ()))
+
+
+def mm(a, b, dims=(((1,), (0,)), ((), ()))):
+    return lax.dot_general(a, b, dims, preferred_element_type=F32)
+
+
+def exact(a, b, dims=(((1,), (0,)), ((), ()))):
+    return lax.dot_general(
+        a, b, dims, preferred_element_type=F32, precision=lax.Precision.HIGHEST
+    )
+
+
+def split2(a):
+    high = a.astype(BF16)
+    return high, (a - high.astype(F32)).astype(BF16)
+
+
+def silu(a):
+    return a / (1.0 + jnp.exp(-a))
+
+
+def decay_rows(decay_ref):
+    heads, length = decay_ref.shape
+    row = lax.broadcasted_iota(jnp.int32, (length, length), 0)
+    col = lax.broadcasted_iota(jnp.int32, (length, length), 1)
+    return exact(decay_ref[...], (row <= col).astype(F32)), row, col
+
+
+def spread(values):
+    high, low = split2(jnp.broadcast_to(values, (values.shape[0], LANES)))
+    rest = PAD - 2 * values.shape[0]
+    return jnp.concatenate([high, low, jnp.zeros((rest, LANES), BF16)], axis=0)
+
+
+def state_kernel(place_ref, keys_ref, values_ref, decay_ref, sent_ref, kept_ref, own_ref, all_ref, dec_ref):
+    heads, length = decay_ref.shape
+    half = heads // 2
+    cum, _, _ = decay_rows(decay_ref)
+    total = cum[:, length - 1 :]
+    tail = jnp.transpose(jnp.exp(total - cum))
+    whole = jnp.exp(total)
+    for h in range(heads):
+        lanes = pl.ds(h * LANES, LANES)
+        act = silu(keys_ref[:, lanes].astype(F32)) * tail[:, h : h + 1]
+        high, low = split2(act)
+        value = values_ref[:, lanes]
+        all_ref[h] = mm(high, value, TN) + mm(low, value, TN)
+    dec_ref[0] = jnp.broadcast_to(whole[:half], (half, LANES))
+    dec_ref[1] = jnp.broadcast_to(whole[half:], (half, LANES))
+    mine = place_ref[0] % 2
+    for i in range(half):
+        sent_ref[pl.ds(i * LANES, LANES), :] = all_ref[(1 - mine) * half + i].astype(BF16)
+        kept_ref[i] = all_ref[mine * half + i]
+    sent_ref[pl.ds(half * LANES, PAD), :] = spread(dec_ref[1 - mine])
+    own_ref[...] = dec_ref[mine]
+
+
+def inner_kernel(
+    queries_ref, keys_ref, values_ref, decay_ref, gain_ref, gate_ref, inner_ref, high_ref, low_ref, gate_out_ref
+):
+    heads, length = decay_ref.shape
+    cum, row, col = decay_rows(decay_ref)
+    columns = jnp.transpose(cum)
+    grown = jnp.exp(columns)
+    causal = row >= col
+    for h in range(heads):
+        lanes = pl.ds(h * LANES, LANES)
+        query = silu(queries_ref[:, lanes].astype(F32))
+        high_ref[:, lanes], low_ref[:, lanes] = split2(query * grown[:, h : h + 1])
+        q_high, q_low = split2(query)
+        k_high, k_low = split2(silu(keys_ref[:, lanes].astype(F32)))
+        gap = jnp.where(causal, columns[:, h : h + 1] - cum[h : h + 1, :], 0.0)
+        weight = jnp.where(causal, jnp.exp(gap), 0.0)
+        scores = (mm(q_high, k_high, NT) + (mm(q_high, k_low, NT) + mm(q_low, k_high, NT))) * weight
+        high, low = split2(scores)
+        value = values_ref[:, lanes]
+        inner_ref[:, lanes] = mm(high, value) + mm(low, value)
+        gate = 1.0 / (1.0 + jnp.exp(-gate_ref[:, lanes].astype(F32)))
+        gate_out_ref[:, lanes] = gate * gain_ref[:, lanes].astype(F32)
+
+
+def expert_table(routes_ref, count):
+    length = routes_ref.shape[1]
+    ids = lax.broadcasted_iota(jnp.int32, (count, length), 0)
+    first = routes_ref[0:1, :] == ids
+    second = routes_ref[1:2, :] == ids
+    named = jnp.where(first | second, 1.0, 0.0)
+    row = lax.broadcasted_iota(jnp.int32, (length, length), 0)
+    col = lax.broadcasted_iota(jnp.int32, (length, length), 1)
+    rank = mm(named.astype(BF16), jnp.where(row < col, 1.0, 0.0).astype(BF16))
+    return first, second, jnp.where(named > 0.0, rank.astype(jnp.int32), -1)
+
+
+def hidden_kernel(
+    place_ref, high_ref, low_ref, inner_ref, own_ref, other_ref, gate_ref,
+    residual_ref, moe_gain_ref, router_ref, routes_ref, hidden_ref, stats_ref, *rest,
+):
+    packed_refs, rank_ref = rest[:-1], rest[-1]
+    half = own_ref.shape[0]
+    heads, length = 2 * half, inner_ref.shape[0]
+    count, slots = len(packed_refs), packed_refs[0].shape[0]
+    first_half = place_ref[0] % 2 == 0
+    squares = jnp.zeros((length, LANES), F32)
+    logits = jnp.zeros((count, length), F32)
+    for h in range(heads):
+        lanes = pl.ds(h * LANES, LANES)
+        mine, other = own_ref[h % half], other_ref[pl.ds((h % half) * LANES, LANES), :]
+        carry = jnp.where(first_half == (h < half), mine, other)
+        attn = inner_ref[:, lanes] + (mm(high_ref[:, lanes], carry) + mm(low_ref[:, lanes], carry))
+        mean_sq = jnp.mean(attn * attn, axis=1, keepdims=True)
+        gated = attn * lax.rsqrt(mean_sq + 1e-06) * gate_ref[:, lanes]
+        hidden = (residual_ref[:, lanes].astype(F32) + gated).astype(BF16)
+        hidden_ref[:, lanes] = hidden
+        wide = hidden.astype(F32)
+        squares = squares + wide * wide
+        scaled = (wide * moe_gain_ref[:, lanes].astype(F32)).astype(BF16)
+        logits = logits + mm(router_ref[:, lanes], scaled, NT)
+    stats_ref[0:count, :] = logits
+    stats_ref[count:, :] = exact(jnp.ones((8, LANES), F32), squares, NT)
+    _, _, rank = expert_table(routes_ref, count)
+    rank_ref[...] = rank
+    rows = hidden_ref[...]
+    slot = lax.broadcasted_iota(jnp.int32, (slots, length), 0)
+    for k, packed_ref in enumerate(packed_refs):
+        pick = jnp.where(rank_ref[pl.ds(place_ref[0] ^ k, 1), :] == slot, 1.0, 0.0).astype(BF16)
+        packed_ref[...] = mm(pick, rows).astype(BF16)
+
+
+def rows_kernel(moe_gain_ref, *rest):
+    arrived_refs, (rows_ref, squares_ref) = rest[:-2], rest[-2:]
+    capacity, width = arrived_refs[0].shape
+    total = len(arrived_refs) * capacity
+    groups = pl.cdiv(total, LANES)
+    sums = []
+    for s, arrived_ref in enumerate(arrived_refs):
+        wide = arrived_ref[...].astype(F32)
+        rows_ref[pl.ds(s * capacity, capacity), :] = (wide * moe_gain_ref[...].astype(F32)).astype(BF16)
+        square = wide * wide
+        part = square[:, :LANES]
+        for k in range(1, width // LANES):
+            part = part + square[:, k * LANES : (k + 1) * LANES]
+        sums.append(part)
+    sums = jnp.concatenate(sums + [jnp.zeros((groups * LANES - total, LANES), F32)], axis=0)
+    ones = jnp.ones((8, LANES), F32)
+    lines = [exact(ones, sums[g * LANES : (g + 1) * LANES], NT)[0:1] for g in range(groups)]
+    high, low = split2(jnp.concatenate(lines, axis=0))
+    squares_ref[...] = jnp.concatenate(
+        [high, low, jnp.zeros((PAD - 2 * groups, LANES), BF16)], axis=0
+    )
+
+
+def fetch_kernel(jobs, gate_ref, up_ref, down_ref, *rest):
+    targets, sems = rest[:-1], rest[-1]
+    copies = []
+    for n, (which, start, size) in enumerate(jobs):
+        if which == 2:
+            source = down_ref.at[pl.ds(start, size), :]
+        else:
+            source = (gate_ref, up_ref)[which].at[:, pl.ds(start, size)]
+        copies.append(pltpu.make_async_copy(source, targets[n], sems.at[n]))
+    for copy in copies:
+        copy.start()
+    for copy in copies:
+        copy.wait()
+
+
+def chosen(place_ref, other_y, other_core):
+    core, y = place_ref[0] % 2, place_ref[0] // 2
+    return (1 - y if other_y else y) * 2 + (1 - core if other_core else core)
+
+
+def up_part(home, extra, place_ref, rows_ref, squares_ref, *rest):
+    if home:
+        came_ref, gate_ref, up_ref, cross_ref, stay_ref, *more = rest
+    else:
+        gate_ref, up_ref, cross_ref = rest
+    total = rows_ref.shape[0]
+    piece = gate_ref.shape[1] // 4
+    if extra:
+        lines = squares_ref[...]
+        if home:
+            groups = pl.cdiv(total, LANES)
+            seen = came_ref[pl.ds(total, PAD), pl.ds(0, LANES)].astype(F32) + lines.astype(F32)
+            line_sum = seen[:groups] + seen[groups : 2 * groups]
+            more[0][...] = jnp.concatenate([line_sum, jnp.zeros((PAD - groups, LANES), F32)], axis=0)
+            high, low = split2(line_sum)
+            lines = jnp.concatenate([high, low, jnp.zeros((PAD - 2 * groups, LANES), BF16)], axis=0)
+        cross_ref[pl.ds(total, PAD), pl.ds(0, LANES)] = lines
+        left = cross_ref.shape[1] - LANES
+        cross_ref[pl.ds(total, PAD), pl.ds(LANES, left)] = jnp.zeros((PAD, left), BF16)
+    for k in range(2):
+        start = pl.multiple_of(chosen(place_ref, k == 0, not home) * piece, LANES)
+        for i, weights in enumerate((gate_ref, up_ref)):
+            lanes = pl.ds((2 * k + i) * piece, piece)
+            sums = mm(rows_ref[...], weights[:, pl.ds(start, piece)])
+            if home:
+                sums = sums + came_ref[pl.ds(0, total), lanes].astype(F32)
+            if home and k == 1:
+                stay_ref[:, pl.ds(i * piece, piece)] = sums
+            else:
+                cross_ref[pl.ds(0, total), lanes] = sums.astype(BF16)
+
+
+def up_kernel(jobs, place_ref, rows_ref, squares_ref, *refs):
+    counts = [(3 if home else 2, 1 + home + (home and extra)) for home, extra in jobs]
+    inputs, outputs = refs[: sum(n for n, _ in counts)], refs[sum(n for n, _ in counts) :]
+    for (home, extra), (taken, made) in zip(jobs, counts):
+        up_part(home, extra, place_ref, rows_ref, squares_ref, *inputs[:taken], *outputs[:made])
+        inputs, outputs = inputs[taken:], outputs[made:]
+
+
+def act_kernel(full_width, extra, stay_ref, seen_ref, scale_ref, act_ref, *more):
+    total, piece = act_ref.shape
+    if extra:
+        groups = pl.cdiv(total, LANES)
+        lines = seen_ref[pl.ds(total, PAD), pl.ds(0, LANES)].astype(F32)
+        line_sum = scale_ref[0:groups, :] + lines[:groups] + lines[groups : 2 * groups]
+        factor = lax.rsqrt(line_sum / full_width + 1e-06)
+        columns = [jnp.transpose(jnp.broadcast_to(factor[g : g + 1], (8, LANES))) for g in range(groups)]
+        scale = jnp.concatenate(columns, axis=0)[:total]
+        more[0][...] = scale
+        scale = scale[:, 0:1]
+    else:
+        scale = scale_ref[:, 0:1]
+    joined = stay_ref[...] + seen_ref[pl.ds(0, total), :].astype(F32)
+    act_ref[...] = (silu(scale * joined[:, :piece]) * (scale * joined[:, piece:])).astype(BF16)
+
+
+def down_kernel(start, place_ref, *rest):
+    acts, rest = rest[:4], rest[4:]
+    total, (down_ref, *out_refs) = (None, rest) if start else (rest[0][...], rest[1:])
+    piece = acts[0].shape[1]
+    for n in range(4):
+        row = pl.multiple_of(chosen(place_ref, n % 2 == 1, n >= 2) * piece, LANES)
+        term = mm(acts[n][...], down_ref[pl.ds(row, piece), :])
+        total = term if total is None else total + term
+    if out_refs[0].dtype == F32:
+        out_refs[0][...] = total
+    else:
+        for s, out_ref in enumerate(out_refs):
+            capacity = out_ref.shape[0]
+            out_ref[...] = total[s * capacity : (s + 1) * capacity].astype(BF16)
+
+
+def combine_kernel(full_width, place_ref, hidden_ref, stats_ref, routes_ref, *rest):
+    returned_refs, (out_ref, rank_ref, weight_ref) = rest[:-3], rest[-3:]
+    count, slots = len(returned_refs), returned_refs[0].shape[0]
+    length = hidden_ref.shape[0]
+    first, second, rank_ref[...] = expert_table(routes_ref, count)
+    scale = lax.rsqrt(stats_ref[count : count + 1, :] / full_width + 1e-06)
+    logits = stats_ref[0:count, :] * scale
+    gap = jnp.sum(jnp.where(first, logits, 0.0), axis=0, keepdims=True) - jnp.sum(
+        jnp.where(second, logits, 0.0), axis=0, keepdims=True
+    )
+    weight_ref[...] = jnp.where(first, 1.0 / (1.0 + jnp.exp(-gap)), 1.0 / (1.0 + jnp.exp(gap)))
+    slot = lax.broadcasted_iota(jnp.int32, (slots, length), 0)
+    total = hidden_ref[...].astype(F32)
+    for k, returned_ref in enumerate(returned_refs):
+        line = pl.ds(place_ref[0] ^ k, 1)
+        pick = jnp.where(rank_ref[line, :] == slot, weight_ref[line, :], 0.0)
+        high, low = split2(pick)
+        total = total + mm(high, returned_ref[...], TN) + mm(low, returned_ref[...], TN)
+    out_ref[...] = total.astype(BF16)
+
+
+LIGHT = 1
+VMEM = pl.BlockSpec(memory_space=pltpu.VMEM)
+SMEM = pl.BlockSpec(memory_space=pltpu.SMEM)
+ANY = pl.BlockSpec(memory_space=pl.ANY)
+
+
+def call(kernel, outs, specs, scratch=(), flops=0, moved=0, room=6):
+    shapes = [jax.ShapeDtypeStruct(*out) for out in outs]
+    single = len(shapes) == 1
+    return pl.pallas_call(
+        kernel,
+        out_shape=shapes[0] if single else shapes,
+        in_specs=specs,
+        out_specs=VMEM if single else [VMEM] * len(shapes),
+        scratch_shapes=list(scratch),
+        cost_estimate=pl.CostEstimate(flops=flops // LIGHT, bytes_accessed=moved // LIGHT, transcendentals=0),
+        compiler_params=pltpu.CompilerParams(vmem_limit_bytes=room << 20),
+    )
+
+
+def pinned(array):
+    return pltpu.with_memory_space_constraint(array, pltpu.HBM)
+
+
+def after_all(value, *others):
+    return lax.optimization_barrier((value,) + others)[0]
+
+
+def flip(count, bit):
+    return [(i, i ^ bit) for i in range(count)]
+
+
+def shift(count, step):
+    return [(i, i + step) for i in range(count - step)]
+
+
+def unpack(message, half):
+    state = message[: half * LANES].astype(F32).reshape(half, LANES, LANES)
+    lines = message[half * LANES :].astype(F32)
+    return state, (lines[:half] + lines[half : 2 * half])[:, None, :]
+
+
+def pack(state, decay):
+    half = state.shape[0]
+    return jnp.concatenate([state.astype(BF16).reshape(half * LANES, LANES), spread(decay[:, 0, :])])
+
+
+UNITS = (3, 4, 2)
+FETCH = tuple((name, c) for name in "gud" for c in range(len(UNITS)))
+GROUPS = ((0, 1, 2, 3, 4, 5, 6, 7),)
+
+
+def local_fast(
+    queries, keys, values, log_decay, out_gate, attn_gain, residual, moe_gain, router, routes,
+    w_gate, w_up, w_down,
+):
+    length, width = queries.shape
+    heads = log_decay.shape[1]
+    half = heads // 2
+    spots, parts = lax.axis_size("seq"), lax.axis_size("head")
+    place, part = lax.axis_index("seq"), lax.axis_index("head")
+    count = router.shape[1]
+    capacity = 2 * length // count + max(1, length // 32)
+    hidden_units = w_gate.shape[1]
+    decay_t, routes_t, router_t = log_decay.T, routes.T, router.T
+    gain_row, moe_row = attn_gain.reshape(1, width), moe_gain.reshape(1, width)
+    spot = place.astype(jnp.int32).reshape(1)
+
+    head_flops = 2 * length * LANES * LANES * heads
+    sent, kept, own_decay = call(
+        state_kernel,
+        [((half * LANES + PAD, LANES), BF16), ((half, LANES, LANES), F32), ((half, LANES), F32)],
+        [SMEM, VMEM, VMEM, VMEM],
+        [pltpu.VMEM((heads, LANES, LANES), F32), pltpu.VMEM((2, half, LANES), F32)],
+        2 * head_flops,
+        6 * length * width,
+    )(spot, pinned(keys), pinned(values), decay_t)
+    own_decay = own_decay[:, None, :]
+    inner, query_high, query_low, gate = call(
+        inner_kernel,
+        [((length, width), F32), ((length, width), BF16), ((length, width), BF16), ((length, width), F32)],
+        [VMEM] * 6,
+        (),
+        5 * head_flops,
+        20 * length * width,
+    )(pinned(queries), pinned(keys), pinned(values), decay_t, gain_row, pinned(out_gate))
+
+    gates, ups, downs = {}, {}, {}
+
+    def fetch(names, token):
+        jobs, shapes = [], []
+        for name, c in names:
+            span = spans[c]
+            size = span.stop - span.start
+            jobs.append(("gud".index(name), span.start, size))
+            shapes.append(pltpu.VMEM((size, width) if name == "d" else (width, size), BF16))
+        moved = pl.pallas_call(
+            functools.partial(fetch_kernel, jobs),
+            out_shape=shapes,
+            in_specs=[ANY] * 3,
+            out_specs=[VMEM] * len(jobs),
+            scratch_shapes=[pltpu.SemaphoreType.DMA((len(jobs),))],
+            cost_estimate=pl.CostEstimate(flops=0, bytes_accessed=1 << 20, transcendentals=0),
+            compiler_params=pltpu.CompilerParams(vmem_limit_bytes=2 << 20),
+        )(*[pinned(after_all(w, token)) for w in (w_gate, w_up, w_down)])
+        for (name, c), array in zip(names, moved):
+            {"g": gates, "u": ups, "d": downs}[name][c] = array
+        return moved[0]
+
+    even = place % 2 == 0
+    part = part.astype(jnp.int32).reshape(1)
+    chunks = range(len(UNITS))
+    ends = [sum(UNITS[: c + 1]) * parts * LANES for c in chunks]
+    spans = [slice(ends[c - 1] if c else 0, ends[c]) for c in chunks]
+
+    theirs, their_decay = unpack(lax.ppermute(sent, "seq", flip(spots, 1)), half)
+    kept = after_all(kept, inner)
+    block = jnp.where(even, their_decay, 1.0) * kept + jnp.where(even, 1.0, own_decay) * theirs
+    block_decay = own_decay * their_decay
+    carry, between = jnp.zeros_like(block), jnp.ones_like(block_decay)
+    step = 1
+    while 2 * step < spots:
+        window = pack(block + block_decay * carry, block_decay * between)
+        if step == 1:
+            window = after_all(window, moe_row)
+        got, got_decay = unpack(lax.ppermute(window, "seq", shift(spots, 2 * step)), half)
+        carry, between = carry + between * got, between * got_decay
+        step *= 2
+    after = jnp.where(even, own_decay, their_decay) * carry + jnp.where(even, kept, theirs)
+    mine = jnp.where(even, carry, after).astype(BF16)
+    other = jnp.where(even, after, carry).astype(BF16).reshape(half * LANES, LANES)
+    other = lax.ppermute(other, "seq", flip(spots, 1))
+
+    hidden, stats, *packed = call(
+        hidden_kernel,
+        [((length, width), BF16), ((count + 8, length), F32)] + [((capacity, width), BF16)] * spots,
+        [SMEM] + [VMEM] * 10,
+        [pltpu.VMEM((count, length), jnp.int32)],
+        3 * head_flops,
+        16 * length * width,
+    )(
+        spot, query_high, query_low, inner, mine, other, gate, pinned(residual),
+        moe_row, pinned(router_t), pinned(routes_t),
+    )
+    def exchange(block, k):
+        return lax.ppermute(block, "seq", flip(spots, k)) if k else block
+
+    arrived = [exchange(block, k) for k, block in enumerate(packed)]
+    sizes = [capacity * len(group) for group in GROUPS]
+    pieces = [size * LANES for size in UNITS]
+    state = {}
+    turn = [hidden]
+
+    def next_turn(value):
+        return after_all(value, turn[-1])
+
+    def gather(g):
+        rows, squares = call(
+            rows_kernel,
+            [((sizes[g], width), BF16), ((PAD, LANES), BF16)],
+            [VMEM] * (1 + len(GROUPS[g])),
+            (),
+            0,
+            4 * sizes[g] * width,
+        )(next_turn(moe_row), *[arrived[k] for k in GROUPS[g]])
+        state["rows", g], state["squares", g] = rows, squares
+        turn.append(rows)
+
+    def up(g, *parts_of):
+        size = sizes[g]
+        outs, inputs, jobs = [], [], []
+        for c, home in parts_of:
+            extra, piece = c == 0, pieces[c]
+            outs.append(((size + PAD * extra, (2 if home else 4) * piece), BF16))
+            if home:
+                outs.append(((size, 2 * piece), F32))
+                inputs.append(state["came", g, c])
+                if extra:
+                    outs.append(((PAD, LANES), F32))
+            inputs += [gates[c], ups[c]]
+            jobs.append((home, extra))
+        made = call(
+            functools.partial(up_kernel, jobs),
+            outs,
+            [SMEM] + [VMEM] * (2 + len(inputs)),
+            (),
+            8 * size * width * sum(pieces[c] for c, _ in parts_of),
+            8 * size * width,
+        )(part, next_turn(state["rows", g]), state["squares", g], *inputs)
+        made = [made] if len(outs) == 1 else list(made)
+        turn.append(made[0])
+        for (c, home), (_, extra) in zip(parts_of, jobs):
+            cross = made.pop(0)
+            if home:
+                state["stay", g, c] = made.pop(0)
+                if extra:
+                    state["lines", g] = made.pop(0)
+                state["seen", g, c] = lax.ppermute(cross, "head", flip(parts, 2))
+            else:
+                state["came", g, c] = lax.ppermute(cross, "head", flip(parts, 1))
+
+    def act(g, c):
+        size, piece, extra = sizes[g], pieces[c], c == 0
+        made = call(
+            functools.partial(act_kernel, float(width * parts), extra),
+            [((size, piece), BF16)] + [((size, 8), F32)] * extra,
+            [VMEM] * 3,
+            (),
+            0,
+            10 * size * piece,
+        )(
+            next_turn(state["stay", g, c]),
+            state["seen", g, c],
+            state["lines" if extra else "scale", g],
+        )
+        if extra:
+            made, state["scale", g] = made
+        across = lax.ppermute(made, "head", flip(parts, 2))
+        beside = lax.ppermute(made, "head", flip(parts, 1))
+        state["acts", g, c] = [made, across, beside]
+        turn.append(made)
+
+    def down(g, c):
+        size, piece, last = sizes[g], pieces[c], c == chunks[-1]
+        made, across, beside = state["acts", g, c]
+        diagonal = lax.ppermute(across, "head", flip(parts, 1))
+        acc = state.get(("acc", g))
+        out = call(
+            functools.partial(down_kernel, c == 0),
+            [((capacity, width), BF16)] * len(GROUPS[g]) if last else [((size, width), F32)],
+            [SMEM] + [VMEM] * (5 + (c > 0)),
+            (),
+            8 * size * width * piece,
+            8 * size * width,
+        )(part, next_turn(made), across, beside, diagonal, *([acc] if c else []), downs[c])
+        state["acc", g] = out
+        turn.append(out[0] if last else out)
+        if last:
+            for k, block in zip(GROUPS[g], out):
+                returned[k] = exchange(block, k)
+
+    def late_fetch():
+        turn.append(fetch(FETCH, turn[-1]))
+
+    returned = {}
+    for job, *where in PLAN:
+        {"gather": gather, "up": up, "act": act, "down": down, "fetch": late_fetch}[job](*where)
+    stats = lax.psum(next_turn(stats), "head")
+    return call(
+        functools.partial(combine_kernel, float(width * parts)),
+        [((length, width), BF16)],
+        [SMEM] + [VMEM] * (3 + spots),
+        [pltpu.VMEM((count, length), jnp.int32), pltpu.VMEM((count, length), F32)],
+        4 * length * count * capacity * width,
+        8 * length * width,
+    )(spot, hidden, stats, pinned(routes_t), *[returned[k] for k in range(spots)])
+
+
+PLAN = (
+    ("fetch",),
+    ("gather", 0),
+    ("up", 0, (0, False)),
+    ("up", 0, (0, True), (1, False)),
+    ("up", 0, (1, True), (2, False)),
+    ("up", 0, (2, True)),
+    ("act", 0, 0),
+    ("act", 0, 1),
+    ("act", 0, 2),
+    ("down", 0, 0),
+    ("down", 0, 1),
+    ("down", 0, 2),
+)
+
+
+def local(*args):
+    queries, log_decay, router, w_gate = args[0], args[3], args[8], args[10]
+    spots, parts = lax.axis_size("seq"), lax.axis_size("head")
+    heads = log_decay.shape[1]
+    fits = (
+        router.shape[1] == spots == sum(map(len, GROUPS))
+        and parts == 4
+        and heads % 2 == 0
+        and queries.shape == (LANES, heads * LANES)
+        and w_gate.shape[1] == sum(UNITS) * parts * LANES
+    )
+    return local_fast(*args) if fits else local_general(*args)
+
+
 def solution(mesh):
     return jax.shard_map(
         local,

time: 357 us -> 173 us (0.48)
  waiting for transfers between devices: 210 us -> 77.3 us
  blocking collectives: 58 us -> 6.03 us
  Pallas kernels: 0 us -> 44.7 us
  matrix products: 41.4 us -> 0 us
  starting transfers between devices: 6.39 us -> 38.3 us
  other arithmetic: 17.1 us -> 0.74 us
  between operations: 13.4 us -> 0.31 us
    all_gather x2 -> x0, waiting for transfers between devices: 99.8 us -> none  [the longest x1 73.9 us: prefix_2(): pieces = jax.tree.map(lambda part: lax.all_gather(part, axis), value)]
    reduce_scatter x2 -> x0, waiting for transfers between devices: 93.7 us -> none  [the longest x1 54.2 us: local(): upward = lax.psum_scatter(up_part, 'head', scatter_dimension=1, tiled=True)]
    ppermute x0 -> x33, waiting for transfers between devices: none -> 77.3 us  [the longest x3 26.9 us: up(): state['seen', g, c] = lax.ppermute(cross, 'head', flip(parts, 2))]
    pallas_call x0 -> x16, Pallas kernels: none -> 44.7 us  [the longest x1 13.4 us: fetch(): pl.pallas_call(functools.partial(fetch_kernel, jobs), out_shape=shapes, i...]
    dot_general x10 -> x0, matrix products: 41.4 us -> none  [the longest x1 11.2 us: local(): up_part = jnp.dot(flat_rows, w_up, preferred_element_type=jnp.float32)]
    ppermute x0 -> x33, starting transfers between devices: none -> 38.3 us  [the longest x14 19.8 us: exchange(): return lax.ppermute(block, 'seq', flip(spots, k)) if k else block]
    all_to_all x1 -> x0, blocking collectives: 28 us -> none  [local(): lax.all_to_all(outgoing, 'seq', split_axis=0, concat_axis=0, tiled=True)]
    all_gather x1 -> x0, blocking collectives: 18.4 us -> none  [prefix_2(): pieces = jax.tree.map(lambda part: lax.all_gather(part, axis), value)]
  transfers between devices with their start and end apart: 5 -> 33, of which waited for: 5 -> 15; matrix products, arithmetic and copies ran while one was open for 5% -> 1% of each run, Pallas kernels for 0% -> 14%
where the time goes in v1:
time: 173 us; the launch traced here: 172 us
  waiting for transfers between devices  77.3 us (45%)
  Pallas kernels  44.7 us (26%)
  starting transfers between devices  38.3 us (22%)
  blocking collectives  6.03 us (3%)
  local copies, waits for them, and re-layouts  4.86 us (3%)
    ppermute x3, waiting for transfers between devices, up(): state['seen', g, c] = lax.ppermute(cross, 'head', flip(parts, 2))  26.9 us
    ppermute x14, starting transfers between devices, exchange(): return lax.ppermute(block, 'seq', flip(spots, k)) if k else block  19.8 us
    ppermute x14, waiting for transfers between devices, exchange(): return lax.ppermute(block, 'seq', flip(spots, k)) if k else block  14.5 us
    pallas_call x1, Pallas kernels, fetch(): pl.pallas_call(functools.partial(fetch_kernel, jobs), out_shape=shapes, i...  13.4 us
    ppermute x3, waiting for transfers between devices, act(): across = lax.ppermute(made, 'head', flip(parts, 2))  12.5 us
    ppermute x2, waiting for transfers between devices, local_fast(): lax.ppermute(window, 'seq', shift(spots, 2 * step))  11.9 us
    pallas_call x4, Pallas kernels, up(): call(functools.partial(up_kernel, jobs), outs, [SMEM] + [VMEM] * (2 + len...  9.96 us
    ppermute x2, starting transfers between devices, local_fast(): lax.ppermute(window, 'seq', shift(spots, 2 * step))  8.17 us
  transfers between devices with their start and end apart: 33, of which 15 were waited for; matrix products, arithmetic and copies ran while one was open for 1% of the time, Pallas kernels for 14%

profile of v1, /device:TPU:8, one launch (start us, length us, event | category | flops | bytes accessed | tf_op | source)
XLA Modules:
  0.0 172.3 jit_solution(13159497448603618094)
XLA Ops:
  0.7 2.3 %shard_map.128 = (bf16[784,128]{1,0:T(8,128)(2,1)S(1)}, f32[6,128,128]{2,1,0:T(8,128)S(1)}, f32[6,128]{1,0:T(8,128)S(1)}) custom-call(s32[1]{0:T(128)} %bitcast.place_ref, bf16[128,1536]{1,0:T(8,128)(2,1)} %keys_ref.3, bf16[128,1536]{1,0:T(8,128)(2,1)} %values_ref.3, f32[12,128]{1,0:T(8,128)S(1)} %bitcast.14), custom_call_target="tpu_custom_call" | custom-call | flops 100663296 | bytes 1179648 | tf_op jit(solution)/shard_map/pallas_call | solution.py:500
  6.6 4.6 %shard_map.127 = (f32[128,1536]{1,0:T(8,128)S(1)}, bf16[128,1536]{1,0:T(8,128)(2,1)S(1)}, bf16[128,1536]{1,0:T(8,128)(2,1)S(1)}, f32[128,1536]{1,0:T(8,128)S(1)}) custom-call(bf16[128,1536]{1,0:T(8,128)(2,1)} %queries_ref.1, bf16[128,1536]{1,0:T(8,128)(2,1)} %keys_ref.3, bf16[128,1536]{1,0:T(8,128)(2,1)} %values_ref.3, f32[12,128]{1,0:T(8,128)S(1)} %bitcast.15, ...), custom_call_target="tpu_custom_call" | custom-call | flops 251658240 | bytes 3932160 | tf_op jit(solution)/shard_map/pallas_call | solution.py:509
  11.7 3.5 %collective-permute-start.1 = (bf16[784,128]{1,0:T(8,128)(2,1)S(1)}, bf16[784,128]{1,0:T(8,128)(2,1)S(1)}, u32[]{:S(2)}, u32[]{:S(2)}) collective-permute-start(bf16[784,128]{1,0:T(8,128)(2,1)S(1)} %maximum_maximum_fusion), channel_id=1, source_target_pairs={{0,8},{4,12},{8,16},{12,20},{16,24},{20,28},{1,9},{5,13},{9,17},{1... | collective-permute-start | bytes 602120 | tf_op jit(solution)/shard_map/ppermute | solution.py:556
  15.2 4.9 %collective-permute-done.1 = bf16[784,128]{1,0:T(8,128)(2,1)S(1)} collective-permute-done((bf16[784,128]{1,0:T(8,128)(2,1)S(1)}, bf16[784,128]{1,0:T(8,128)(2,1)S(1)}, u32[]{:S(2)}, u32[]{:S(2)}) %collective-permute-start.1) | collective-permute-done | bytes 200736 | tf_op jit(solution)/shard_map/ppermute | solution.py:556
  20.4 4.7 %collective-permute-start.2 = (bf16[784,128]{1,0:T(8,128)(2,1)S(1)}, bf16[784,128]{1,0:T(8,128)(2,1)S(1)}, u32[]{:S(2)}, u32[]{:S(2)}) collective-permute-start(bf16[784,128]{1,0:T(8,128)(2,1)S(1)} %maximum_maximum_fusion.1), channel_id=1, source_target_pairs={{0,16},{4,20},{8,24},{12,28},{1,17},{5,21},{9,25},{13,29},{2,18},{... | collective-permute-start | bytes 602120 | tf_op jit(solution)/shard_map/ppermute | solution.py:556
  25.1 7.1 %collective-permute-done.2 = bf16[784,128]{1,0:T(8,128)(2,1)S(1)} collective-permute-done((bf16[784,128]{1,0:T(8,128)(2,1)S(1)}, bf16[784,128]{1,0:T(8,128)(2,1)S(1)}, u32[]{:S(2)}, u32[]{:S(2)}) %collective-permute-start.2) | collective-permute-done | bytes 200736 | tf_op jit(solution)/shard_map/ppermute | solution.py:556
  32.9 6.3 %collective-permute-done.3.other_ref = bf16[768,128]{1,0:T(8,128)(2,1)S(1)} collective-permute-done((bf16[768,128]{1,0:T(8,128)(2,1)S(1)}, bf16[768,128]{1,0:T(8,128)(2,1)S(1)}, u32[]{:S(2)}, u32[]{:S(2)}) %collective-permute-start.3) | collective-permute-done | bytes 196640 | tf_op jit(solution)/shard_map/ppermute | solution.py:562
  39.2 3.1 %shard_map.129 = (bf16[128,1536]{1,0:T(8,128)(2,1)S(1)}, f32[16,128]{1,0:T(8,128)S(1)}, bf16[36,1536]{1,0:T(8,128)(2,1)S(1)}, bf16[36,1536]{1,0:T(8,128)(2,1)S(1...) custom-call(s32[1]{0:T(128)} %bitcast.place_ref, ...), custom_call_target="tpu_custom_call" | custom-call | flops 150994944 | bytes 3145728 | tf_op jit(solution)/shard_map/pallas_call | solution.py:564
  43.5 2.9 %collective-permute-start.6 = (bf16[36,1536]{1,0:T(8,128)(2,1)}, bf16[36,1536]{1,0:T(8,128)(2,1)}, u32[]{:S(2)}, u32[]{:S(2)}) collective-permute-start(bf16[36,1536]{1,0:T(8,128)(2,1)} %get-tuple-element.88), channel_id=1, source_target_pairs={{0,12},{4,8},{8,4},{12,0},{16,28},{20,24},{24,20},{28,16},{1,13},{... | collective-permute-start | bytes 331784 | tf_op jit(solution)/shard_map/ppermute | solution.py:576
  46.5 3.4 %collective-permute-start.7 = (bf16[36,1536]{1,0:T(8,128)(2,1)}, bf16[36,1536]{1,0:T(8,128)(2,1)}, u32[]{:S(2)}, u32[]{:S(2)}) collective-permute-start(bf16[36,1536]{1,0:T(8,128)(2,1)} %get-tuple-element.89), channel_id=1, source_target_pairs={{0,16},{4,20},{8,24},{12,28},{16,0},{20,4},{24,8},{28,12},{1,17},{... | collective-permute-start | bytes 331784 | tf_op jit(solution)/shard_map/ppermute | solution.py:576
  54.1 13.4 %shard_map.130 = (bf16[1536,1536]{1,0:T(8,128)(2,1)S(1)}, bf16[1536,2048]{1,0:T(8,128)(2,1)S(1)}, bf16[1536,1024]{1,0:T(8,128)(2,1)S(1)}, bf16[1536,1536]{1,0:T(...) custom-call(bf16[1536,4608]{1,0:T(8,128)(2,1)} %gate_ref.2, ...), custom_call_target="tpu_custom_call" | custom-call | bytes 1048576 | tf_op jit(solution)/shard_map/pallas_call | solution.py:527
  74.0 2.5 %collective-permute-done.11.refs_0_ = bf16[304,1536]{1,0:T(8,128)(2,1)S(1)} collective-permute-done((bf16[304,1536]{1,0:T(8,128)(2,1)S(1)}, bf16[304,1536]{1,0:T(8,128)(2,1)S(1)}, u32[]{:S(2)}, u32[]{:S(2)}) %collective-permute-start.11) | collective-permute-done | bytes 933920 | tf_op jit(solution)/shard_map/ppermute | solution.py:630
  76.5 3.8 %shard_map.133 = (bf16[304,768]{1,0:T(8,128)(2,1)S(1)}, f32[288,768]{1,0:T(8,128)S(1)}, f32[16,128]{1,0:T(8,128)S(1)}, bf16[288,2048]{1,0:T(8,128)(2,1)S(1)}) custom-call(s32[1]{0:T(128)} %bitcast.12.place_ref, bf16[288,1536]{1,0:T(8,128)(2,1)S(1)} %get-tuple-element.106.rows_ref, bf16[16,128]{1,0:T(8,128)(2,1)S(1)} %get-tuple-element.95.squares_ref, ...), custom_call_target="tpu_custom_call" | custom-call | flops 3170893824 | bytes 3538944 | tf_op jit(solution)/shard_map/pallas_call | solution.py:612
  80.5 2.7 %collective-permute-done.12.refs_0_ = bf16[288,2048]{1,0:T(8,128)(2,1)S(1)} collective-permute-done((bf16[288,2048]{1,0:T(8,128)(2,1)S(1)}, bf16[288,2048]{1,0:T(8,128)(2,1)S(1)}, u32[]{:S(2)}, u32[]{:S(2)}) %collective-permute-start.12) | collective-permute-done | bytes 1179680 | tf_op jit(solution)/shard_map/ppermute | solution.py:630
  83.2 3.0 %shard_map.134 = (bf16[288,1024]{1,0:T(8,128)(2,1)S(1)}, f32[288,1024]{1,0:T(8,128)S(1)}, bf16[288,1024]{1,0:T(8,128)(2,1)S(1)}) custom-call(s32[1]{0:T(128)} %bitcast.12.place_ref, bf16[288,1536]{1,0:T(8,128)(2,1)S(1)} %get-tuple-element.106.rows_ref, bf16[16,128]{1,0:T(8,128)(2,1)S(1)} %get-tuple-element.95.squares_ref, ...), custom_call_target="tpu_custom_call" | custom-call | flops 2717908992 | bytes 3538944 | tf_op jit(solution)/shard_map/pallas_call | solution.py:612
  89.5 22.5 %collective-permute-done.14.seen_ref = bf16[304,768]{1,0:T(8,128)(2,1)S(1)} collective-permute-done((bf16[304,768]{1,0:T(8,128)(2,1)S(1)}, bf16[304,768]{1,0:T(8,128)(2,1)S(1)}, u32[]{:S(2)}, u32[]{:S(2)}) %collective-permute-start.14) | collective-permute-done | bytes 466976 | tf_op jit(solution)/shard_map/ppermute | solution.py:628
  116.3 11.1 %collective-permute-done.17.rest_1_ = bf16[288,384]{1,0:T(8,128)(2,1)S(1)} collective-permute-done((bf16[288,384]{1,0:T(8,128)(2,1)S(1)}, bf16[288,384]{1,0:T(8,128)(2,1)S(1)}, u32[]{:S(2)}, u32[]{:S(2)}) %collective-permute-start.17) | collective-permute-done | bytes 221216 | tf_op jit(solution)/shard_map/ppermute | solution.py:648
  127.9 4.4 %collective-permute-done.16.seen_ref = bf16[288,512]{1,0:T(8,128)(2,1)S(1)} collective-permute-done((bf16[288,512]{1,0:T(8,128)(2,1)S(1)}, bf16[288,512]{1,0:T(8,128)(2,1)S(1)}, u32[]{:S(2)}, u32[]{:S(2)}) %collective-permute-start.16) | collective-permute-done | bytes 294944 | tf_op jit(solution)/shard_map/ppermute | solution.py:628
  134.1 2.2 %shard_map.139.rest_4_ = f32[288,1536]{1,0:T(8,128)S(1)} custom-call(s32[1]{0:T(128)} %bitcast.12.place_ref, bf16[288,384]{1,0:T(8,128)(2,1)S(1)} %get-tuple-element.118.rest_0_, bf16[288,384]{1,0:T(8,128)(2,1)S(1)} %collective-permute-done.17.rest_1_, bf16[288,384]{1,0:T(8,128)(2,1)S(1)} %collective-permute-done.18.rest_2_, ...), custom_call_target="tpu_custom_call" | custom-call | flops 1358954496 | bytes 3538944 | tf_op jit(solution)/shard_map/pallas_call | solution.py:658
  150.9 6.0 %psum.7.stats_ref = f32[16,128]{1,0:T(8,128)S(1)} all-reduce(f32[16,128]{1,0:T(8,128)S(1)} %get-tuple-element.125), channel_id=1, replica_groups=mesh['seq'=8,'head'=4] {'head'}, use_global_device_ids=true, to_apply=%region_0.1 | all-reduce | flops 2048 | bytes 16384 | tf_op jit(solution)/shard_map/psum | solution.py:678
  156.9 3.9 %collective-permute-done.29.rest_4_ = bf16[36,1536]{1,0:T(8,128)(2,1)S(1)} collective-permute-done((bf16[36,1536]{1,0:T(8,128)(2,1)S(1)}, bf16[36,1536]{1,0:T(8,128)(2,1)S(1)}, u32[]{:S(2)}, u32[]{:S(2)}) %collective-permute-start.29) | collective-permute-done | bytes 110624 | tf_op jit(solution)/shard_map/ppermute | solution.py:576
  160.9 2.6 %collective-permute-done.30.rest_5_ = bf16[36,1536]{1,0:T(8,128)(2,1)S(1)} collective-permute-done((bf16[36,1536]{1,0:T(8,128)(2,1)S(1)}, bf16[36,1536]{1,0:T(8,128)(2,1)S(1)}, u32[]{:S(2)}, u32[]{:S(2)}) %collective-permute-start.30) | collective-permute-done | bytes 110624 | tf_op jit(solution)/shard_map/ppermute | solution.py:576
  163.5 3.7 %collective-permute-done.31.rest_6_ = bf16[36,1536]{1,0:T(8,128)(2,1)S(1)} collective-permute-done((bf16[36,1536]{1,0:T(8,128)(2,1)S(1)}, bf16[36,1536]{1,0:T(8,128)(2,1)S(1)}, u32[]{:S(2)}, u32[]{:S(2)}) %collective-permute-start.31) | collective-permute-done | bytes 110624 | tf_op jit(solution)/shard_map/ppermute | solution.py:576
  168.9 3.4 %shard_map.142 = bf16[128,1536]{1,0:T(8,128)(2,1)} custom-call(s32[1]{0:T(128)} %bitcast.place_ref, bf16[128,1536]{1,0:T(8,128)(2,1)S(1)} %get-tuple-element.78.hidden_ref, f32[16,128]{1,0:T(8,128)S(1)} %psum.7.stats_ref, s32[2,128]{1,0:T(2,128)} %bitcast.27, bf16[36,1536]{1,0:T(8,128)(2,1)S(1)} %get-tuple-element.124.rest_0_, ...), custom_call_target="tpu_custom_call" | custom-call | flops 226492416 | bytes 1572864 | tf_op jit(solution)/shard_map/pallas_call | solution.py:679
  (93 shorter events, 43.9 us)
Async XLA Ops:
  3.0 8.4 %collective-permute-start = (bf16[784,128]{1,0:T(8,128)(2,1)S(1)}, bf16[784,128]{1,0:T(8,128)(2,1)S(1)}, u32[]{:S(2)}, u32[]{:S(2)}) collective-permute-start(bf16[784,128]{1,0:T(8,128)(2,1)S(1)} %get-tuple-element.72), channel_id=1, source_target_pairs={{0,4},{4,0},{8,12},{12,8},{16,20},{20,16},{24,28},{28,24},{1,5},{5... | collective-permute-start | bytes 602120 | tf_op jit(solution)/shard_map/ppermute | solution.py:546
  11.7 8.3 %collective-permute-start.1 = (bf16[784,128]{1,0:T(8,128)(2,1)S(1)}, bf16[784,128]{1,0:T(8,128)(2,1)S(1)}, u32[]{:S(2)}, u32[]{:S(2)}) collective-permute-start(bf16[784,128]{1,0:T(8,128)(2,1)S(1)} %maximum_maximum_fusion), channel_id=1, source_target_pairs={{0,8},{4,12},{8,16},{12,20},{16,24},{20,28},{1,9},{5,13},{9,17},{1... | collective-permute-start | bytes 602120 | tf_op jit(solution)/shard_map/ppermute | solution.py:556
  20.4 11.8 %collective-permute-start.2 = (bf16[784,128]{1,0:T(8,128)(2,1)S(1)}, bf16[784,128]{1,0:T(8,128)(2,1)S(1)}, u32[]{:S(2)}, u32[]{:S(2)}) collective-permute-start(bf16[784,128]{1,0:T(8,128)(2,1)S(1)} %maximum_maximum_fusion.1), channel_id=1, source_target_pairs={{0,16},{4,20},{8,24},{12,28},{1,17},{5,21},{9,25},{13,29},{2,18},{... | collective-permute-start | bytes 602120 | tf_op jit(solution)/shard_map/ppermute | solution.py:556
  43.5 8.5 %collective-permute-start.5 = (bf16[36,1536]{1,0:T(8,128)(2,1)S(1)}, bf16[36,1536]{1,0:T(8,128)(2,1)S(1)}, u32[]{:S(2)}, u32[]{:S(2)}) collective-permute-start(bf16[36,1536]{1,0:T(8,128)(2,1)S(1)} %get-tuple-element.87), channel_id=1, source_target_pairs={{0,8},{4,12},{8,0},{12,4},{16,24},{20,28},{24,16},{28,20},{1,9},{5... | collective-permute-start | bytes 331784 | tf_op jit(solution)/shard_map/ppermute | solution.py:576
  43.5 23.9 %collective-permute-start.6 = (bf16[36,1536]{1,0:T(8,128)(2,1)}, bf16[36,1536]{1,0:T(8,128)(2,1)}, u32[]{:S(2)}, u32[]{:S(2)}) collective-permute-start(bf16[36,1536]{1,0:T(8,128)(2,1)} %get-tuple-element.88), channel_id=1, source_target_pairs={{0,12},{4,8},{8,4},{12,0},{16,28},{20,24},{24,20},{28,16},{1,13},{... | collective-permute-start | bytes 331784 | tf_op jit(solution)/shard_map/ppermute | solution.py:576
  46.5 21.0 %collective-permute-start.7 = (bf16[36,1536]{1,0:T(8,128)(2,1)}, bf16[36,1536]{1,0:T(8,128)(2,1)}, u32[]{:S(2)}, u32[]{:S(2)}) collective-permute-start(bf16[36,1536]{1,0:T(8,128)(2,1)} %get-tuple-element.89), channel_id=1, source_target_pairs={{0,16},{4,20},{8,24},{12,28},{16,0},{20,4},{24,8},{28,12},{1,17},{... | collective-permute-start | bytes 331784 | tf_op jit(solution)/shard_map/ppermute | solution.py:576
  49.8 17.6 %collective-permute-start.8 = (bf16[36,1536]{1,0:T(8,128)(2,1)}, bf16[36,1536]{1,0:T(8,128)(2,1)}, u32[]{:S(2)}, u32[]{:S(2)}) collective-permute-start(bf16[36,1536]{1,0:T(8,128)(2,1)} %get-tuple-element.90), channel_id=1, source_target_pairs={{0,20},{4,16},{8,28},{12,24},{16,4},{20,0},{24,12},{28,8},{1,21},{... | collective-permute-start | bytes 331784 | tf_op jit(solution)/shard_map/ppermute | solution.py:576
  50.5 17.9 %collective-permute-start.9 = (bf16[36,1536]{1,0:T(8,128)(2,1)}, bf16[36,1536]{1,0:T(8,128)(2,1)}, u32[]{:S(2)}, u32[]{:S(2)}) collective-permute-start(bf16[36,1536]{1,0:T(8,128)(2,1)} %get-tuple-element.91), channel_id=1, source_target_pairs={{0,24},{4,28},{8,16},{12,20},{16,8},{20,12},{24,0},{28,4},{1,25},{... | collective-permute-start | bytes 331784 | tf_op jit(solution)/shard_map/ppermute | solution.py:576
  52.6 17.4 %collective-permute-start.10 = (bf16[36,1536]{1,0:T(8,128)(2,1)}, bf16[36,1536]{1,0:T(8,128)(2,1)}, u32[]{:S(2)}, u32[]{:S(2)}) collective-permute-start(bf16[36,1536]{1,0:T(8,128)(2,1)} %get-tuple-element.92), channel_id=1, source_target_pairs={{0,28},{4,24},{8,20},{12,16},{16,12},{20,8},{24,4},{28,0},{1,29},{... | collective-permute-start | bytes 331784 | tf_op jit(solution)/shard_map/ppermute | solution.py:576
  86.4 26.0 %collective-permute-start.15 = (bf16[288,1024]{1,0:T(8,128)(2,1)S(1)}, bf16[288,1024]{1,0:T(8,128)(2,1)S(1)}, u32[]{:S(2)}, u32[]{:S(2)}) collective-permute-start(bf16[288,1024]{1,0:T(8,128)(2,1)S(1)} %get-tuple-element.105), channel_id=1, source_target_pairs={{0,2},{1,3},{2,0},{3,1},{4,6},{5,7},{6,4},{7,5},{8,10},{9,11},{10,... | collective-permute-start | bytes 1769480 | tf_op jit(solution)/shard_map/ppermute | solution.py:628
  87.9 24.2 %collective-permute-start.14 = (bf16[304,768]{1,0:T(8,128)(2,1)S(1)}, bf16[304,768]{1,0:T(8,128)(2,1)S(1)}, u32[]{:S(2)}, u32[]{:S(2)}) collective-permute-start(bf16[304,768]{1,0:T(8,128)(2,1)S(1)} %get-tuple-element.100), channel_id=1, source_target_pairs={{0,2},{1,3},{2,0},{3,1},{4,6},{5,7},{6,4},{7,5},{8,10},{9,11},{10,... | collective-permute-start | bytes 1400840 | tf_op jit(solution)/shard_map/ppermute | solution.py:628
  112.7 15.2 %collective-permute-start.20 = (bf16[288,512]{1,0:T(8,128)(2,1)S(1)}, bf16[288,512]{1,0:T(8,128)(2,1)S(1)}, u32[]{:S(2)}, u32[]{:S(2)}) collective-permute-start(bf16[288,512]{1,0:T(8,128)(2,1)S(1)} %shard_map.137.rest_0_), channel_id=1, source_target_pairs={{0,2},{1,3},{2,0},{3,1},{4,6},{5,7},{6,4},{7,5},{8,10},{9,11},{10,... | collective-permute-start | bytes 884744 | tf_op jit(solution)/shard_map/ppermute | solution.py:648
  114.3 13.1 %collective-permute-start.17 = (bf16[288,384]{1,0:T(8,128)(2,1)S(1)}, bf16[288,384]{1,0:T(8,128)(2,1)S(1)}, u32[]{:S(2)}, u32[]{:S(2)}) collective-permute-start(bf16[288,384]{1,0:T(8,128)(2,1)S(1)} %get-tuple-element.118.rest_0_), channel_id=1, source_target_pairs={{0,2},{1,3},{2,0},{3,1},{4,6},{5,7},{6,4},{7,5},{8,10},{9,11},{10,... | collective-permute-start | bytes 663560 | tf_op jit(solution)/shard_map/ppermute | solution.py:648
  114.8 17.5 %collective-permute-start.16 = (bf16[288,512]{1,0:T(8,128)(2,1)S(1)}, bf16[288,512]{1,0:T(8,128)(2,1)S(1)}, u32[]{:S(2)}, u32[]{:S(2)}) collective-permute-start(bf16[288,512]{1,0:T(8,128)(2,1)S(1)} %get-tuple-element.111), channel_id=1, source_target_pairs={{0,2},{1,3},{2,0},{3,1},{4,6},{5,7},{6,4},{7,5},{8,10},{9,11},{10,... | collective-permute-start | bytes 884744 | tf_op jit(solution)/shard_map/ppermute | solution.py:628
  116.3 17.8 %collective-permute-start.18 = (bf16[288,384]{1,0:T(8,128)(2,1)S(1)}, bf16[288,384]{1,0:T(8,128)(2,1)S(1)}, u32[]{:S(2)}, u32[]{:S(2)}) collective-permute-start(bf16[288,384]{1,0:T(8,128)(2,1)S(1)} %get-tuple-element.118.rest_0_), channel_id=1, source_target_pairs={{0,1},{1,0},{2,3},{3,2},{4,5},{5,4},{6,7},{7,6},{8,9},{9,8},{10,11... | collective-permute-start | bytes 663560 | tf_op jit(solution)/shard_map/ppermute | solution.py:649
  127.4 10.3 %collective-permute-start.21 = (bf16[288,512]{1,0:T(8,128)(2,1)S(1)}, bf16[288,512]{1,0:T(8,128)(2,1)S(1)}, u32[]{:S(2)}, u32[]{:S(2)}) collective-permute-start(bf16[288,512]{1,0:T(8,128)(2,1)S(1)} %shard_map.137.rest_0_), channel_id=1, source_target_pairs={{0,1},{1,0},{2,3},{3,2},{4,5},{5,4},{6,7},{7,6},{8,9},{9,8},{10,11... | collective-permute-start | bytes 884744 | tf_op jit(solution)/shard_map/ppermute | solution.py:649
  127.9 9.8 %collective-permute-start.22 = (bf16[288,512]{1,0:T(8,128)(2,1)S(1)}, bf16[288,512]{1,0:T(8,128)(2,1)S(1)}, u32[]{:S(2)}, u32[]{:S(2)}) collective-permute-start(bf16[288,512]{1,0:T(8,128)(2,1)S(1)} %collective-permute-done.20.rest_1_), channel_id=1, source_target_pairs={{0,1},{1,0},{2,3},{3,2},{4,5},{5,4},{6,7},{7,6},{8,9},{9,8},{10,11... | collective-permute-start | bytes 884744 | tf_op jit(solution)/shard_map/ppermute | solution.py:656
  140.9 7.3 %collective-permute-start.26 = (bf16[36,1536]{1,0:T(8,128)(2,1)S(1)}, bf16[36,1536]{1,0:T(8,128)(2,1)S(1)}, u32[]{:S(2)}, u32[]{:S(2)}) collective-permute-start(bf16[36,1536]{1,0:T(8,128)(2,1)S(1)} %get-tuple-element.126), channel_id=1, source_target_pairs={{0,4},{4,0},{8,12},{12,8},{16,20},{20,16},{24,28},{28,24},{1,5},{5... | collective-permute-start | bytes 331784 | tf_op jit(solution)/shard_map/ppermute | solution.py:576
  142.3 7.8 %collective-permute-start.27 = (bf16[36,1536]{1,0:T(8,128)(2,1)S(1)}, bf16[36,1536]{1,0:T(8,128)(2,1)S(1)}, u32[]{:S(2)}, u32[]{:S(2)}) collective-permute-start(bf16[36,1536]{1,0:T(8,128)(2,1)S(1)} %get-tuple-element.127), channel_id=1, source_target_pairs={{0,8},{4,12},{8,0},{12,4},{16,24},{20,28},{24,16},{28,20},{1,9},{5... | collective-permute-start | bytes 331784 | tf_op jit(solution)/shard_map/ppermute | solution.py:576
  142.3 14.6 %collective-permute-start.28 = (bf16[36,1536]{1,0:T(8,128)(2,1)S(1)}, bf16[36,1536]{1,0:T(8,128)(2,1)S(1)}, u32[]{:S(2)}, u32[]{:S(2)}) collective-permute-start(bf16[36,1536]{1,0:T(8,128)(2,1)S(1)} %get-tuple-element.128), channel_id=1, source_target_pairs={{0,12},{4,8},{8,4},{12,0},{16,28},{20,24},{24,20},{28,16},{1,13},{... | collective-permute-start | bytes 331784 | tf_op jit(solution)/shard_map/ppermute | solution.py:576
  144.4 16.4 %collective-permute-start.29 = (bf16[36,1536]{1,0:T(8,128)(2,1)S(1)}, bf16[36,1536]{1,0:T(8,128)(2,1)S(1)}, u32[]{:S(2)}, u32[]{:S(2)}) collective-permute-start(bf16[36,1536]{1,0:T(8,128)(2,1)S(1)} %get-tuple-element.129), channel_id=1, source_target_pairs={{0,16},{4,20},{8,24},{12,28},{16,0},{20,4},{24,8},{28,12},{1,17},{... | collective-permute-start | bytes 331784 | tf_op jit(solution)/shard_map/ppermute | solution.py:576
  146.6 16.9 %collective-permute-start.30 = (bf16[36,1536]{1,0:T(8,128)(2,1)S(1)}, bf16[36,1536]{1,0:T(8,128)(2,1)S(1)}, u32[]{:S(2)}, u32[]{:S(2)}) collective-permute-start(bf16[36,1536]{1,0:T(8,128)(2,1)S(1)} %get-tuple-element.130), channel_id=1, source_target_pairs={{0,20},{4,16},{8,28},{12,24},{16,4},{20,0},{24,12},{28,8},{1,21},{... | collective-permute-start | bytes 331784 | tf_op jit(solution)/shard_map/ppermute | solution.py:576
  148.2 19.0 %collective-permute-start.31 = (bf16[36,1536]{1,0:T(8,128)(2,1)S(1)}, bf16[36,1536]{1,0:T(8,128)(2,1)S(1)}, u32[]{:S(2)}, u32[]{:S(2)}) collective-permute-start(bf16[36,1536]{1,0:T(8,128)(2,1)S(1)} %get-tuple-element.131), channel_id=1, source_target_pairs={{0,24},{4,28},{8,16},{12,20},{16,8},{20,12},{24,0},{28,4},{1,25},{... | collective-permute-start | bytes 331784 | tf_op jit(solution)/shard_map/ppermute | solution.py:576
  150.2 18.7 %collective-permute-start.32 = (bf16[36,1536]{1,0:T(8,128)(2,1)S(1)}, bf16[36,1536]{1,0:T(8,128)(2,1)S(1)}, u32[]{:S(2)}, u32[]{:S(2)}) collective-permute-start(bf16[36,1536]{1,0:T(8,128)(2,1)S(1)} %get-tuple-element.132), channel_id=1, source_target_pairs={{0,28},{4,24},{8,20},{12,16},{16,12},{20,8},{24,4},{28,0},{1,29},{... | collective-permute-start | bytes 331784 | tf_op jit(solution)/shard_map/ppermute | solution.py:576
  (17 other events, 92.3 us)

commit v2 on v1

--- a/solution.py
+++ b/solution.py
@@ -221,7 +221,7 @@
 
 
 def inner_kernel(
-    queries_ref, keys_ref, values_ref, decay_ref, gain_ref, gate_ref, inner_ref, high_ref, low_ref, gate_out_ref
+    queries_ref, keys_ref, values_ref, decay_ref, inner_ref, high_ref, low_ref
 ):
     heads, length = decay_ref.shape
     cum, row, col = decay_rows(decay_ref)
@@ -240,8 +240,11 @@
         high, low = split2(scores)
         value = values_ref[:, lanes]
         inner_ref[:, lanes] = mm(high, value) + mm(low, value)
-        gate = 1.0 / (1.0 + jnp.exp(-gate_ref[:, lanes].astype(F32)))
-        gate_out_ref[:, lanes] = gate * gain_ref[:, lanes].astype(F32)
+
+
+def gate_kernel(gain_ref, gate_ref, out_ref):
+    gate = 1.0 / (1.0 + jnp.exp(-gate_ref[...].astype(F32)))
+    out_ref[...] = gate * gain_ref[...].astype(F32)
 
 
 def expert_table(routes_ref, count):
@@ -334,44 +337,45 @@
     return (1 - y if other_y else y) * 2 + (1 - core if other_core else core)
 
 
-def up_part(home, extra, place_ref, rows_ref, squares_ref, *rest):
-    if home:
-        came_ref, gate_ref, up_ref, cross_ref, stay_ref, *more = rest
-    else:
-        gate_ref, up_ref, cross_ref = rest
-    total = rows_ref.shape[0]
+def up_part(home, place_ref, rows_ref, gate_ref, up_ref, out_ref):
     piece = gate_ref.shape[1] // 4
-    if extra:
-        lines = squares_ref[...]
-        if home:
-            groups = pl.cdiv(total, LANES)
-            seen = came_ref[pl.ds(total, PAD), pl.ds(0, LANES)].astype(F32) + lines.astype(F32)
-            line_sum = seen[:groups] + seen[groups : 2 * groups]
-            more[0][...] = jnp.concatenate([line_sum, jnp.zeros((PAD - groups, LANES), F32)], axis=0)
-            high, low = split2(line_sum)
-            lines = jnp.concatenate([high, low, jnp.zeros((PAD - 2 * groups, LANES), BF16)], axis=0)
-        cross_ref[pl.ds(total, PAD), pl.ds(0, LANES)] = lines
-        left = cross_ref.shape[1] - LANES
-        cross_ref[pl.ds(total, PAD), pl.ds(LANES, left)] = jnp.zeros((PAD, left), BF16)
     for k in range(2):
         start = pl.multiple_of(chosen(place_ref, k == 0, not home) * piece, LANES)
         for i, weights in enumerate((gate_ref, up_ref)):
             lanes = pl.ds((2 * k + i) * piece, piece)
             sums = mm(rows_ref[...], weights[:, pl.ds(start, piece)])
-            if home:
-                sums = sums + came_ref[pl.ds(0, total), lanes].astype(F32)
-            if home and k == 1:
-                stay_ref[:, pl.ds(i * piece, piece)] = sums
-            else:
-                cross_ref[pl.ds(0, total), lanes] = sums.astype(BF16)
+            out_ref[pl.ds(0, rows_ref.shape[0]), lanes] = sums.astype(out_ref.dtype)
 
 
 def up_kernel(jobs, place_ref, rows_ref, squares_ref, *refs):
-    counts = [(3 if home else 2, 1 + home + (home and extra)) for home, extra in jobs]
-    inputs, outputs = refs[: sum(n for n, _ in counts)], refs[sum(n for n, _ in counts) :]
-    for (home, extra), (taken, made) in zip(jobs, counts):
-        up_part(home, extra, place_ref, rows_ref, squares_ref, *inputs[:taken], *outputs[:made])
-        inputs, outputs = inputs[taken:], outputs[made:]
+    total = rows_ref.shape[0]
+    for n, (home, extra) in enumerate(jobs):
+        out_ref = refs[2 * len(jobs) + n]
+        if extra:
+            left = out_ref.shape[1] - LANES
+            out_ref[pl.ds(total, PAD), pl.ds(0, LANES)] = squares_ref[...]
+            out_ref[pl.ds(total, PAD), pl.ds(LANES, left)] = jnp.zeros((PAD, left), BF16)
+        up_part(home, place_ref, rows_ref, refs[2 * n], refs[2 * n + 1], out_ref)
+
+
+def add_kernel(extra, home_ref, came_ref, squares_ref, cross_ref, stay_ref, *more):
+    total, width = stay_ref.shape
+    for k in range(2):
+        lanes = pl.ds(k * width, width)
+        sums = home_ref[:, lanes] + came_ref[pl.ds(0, total), lanes].astype(F32)
+        if k:
+            stay_ref[...] = sums
+        else:
+            cross_ref[pl.ds(0, total), :] = sums.astype(BF16)
+    if extra:
+        groups = pl.cdiv(total, LANES)
+        seen = came_ref[pl.ds(total, PAD), pl.ds(0, LANES)].astype(F32) + squares_ref[...].astype(F32)
+        line_sum = seen[:groups] + seen[groups : 2 * groups]
+        more[0][...] = jnp.concatenate([line_sum, jnp.zeros((PAD - groups, LANES), F32)], axis=0)
+        high, low = split2(line_sum)
+        lines = jnp.concatenate([high, low, jnp.zeros((PAD - 2 * groups, LANES), BF16)], axis=0)
+        cross_ref[pl.ds(total, PAD), pl.ds(0, LANES)] = lines
+        cross_ref[pl.ds(total, PAD), pl.ds(LANES, width - LANES)] = jnp.zeros((PAD, width - LANES), BF16)
 
 
 def act_kernel(full_width, extra, stay_ref, seen_ref, scale_ref, act_ref, *more):
@@ -475,8 +479,8 @@
     return jnp.concatenate([state.astype(BF16).reshape(half * LANES, LANES), spread(decay[:, 0, :])])
 
 
-UNITS = (3, 4, 2)
-FETCH = tuple((name, c) for name in "gud" for c in range(len(UNITS)))
+UNITS = (2, 4, 3)
+FETCHES = tuple(tuple((name, c) for name in names for c in range(len(UNITS))) for names in ("gu", "d"))
 GROUPS = ((0, 1, 2, 3, 4, 5, 6, 7),)
 
 
@@ -493,7 +497,6 @@
     capacity = 2 * length // count + max(1, length // 32)
     hidden_units = w_gate.shape[1]
     decay_t, routes_t, router_t = log_decay.T, routes.T, router.T
-    gain_row, moe_row = attn_gain.reshape(1, width), moe_gain.reshape(1, width)
     spot = place.astype(jnp.int32).reshape(1)
 
     head_flops = 2 * length * LANES * LANES * heads
@@ -506,14 +509,14 @@
         6 * length * width,
     )(spot, pinned(keys), pinned(values), decay_t)
     own_decay = own_decay[:, None, :]
-    inner, query_high, query_low, gate = call(
+    inner, query_high, query_low = call(
         inner_kernel,
-        [((length, width), F32), ((length, width), BF16), ((length, width), BF16), ((length, width), F32)],
-        [VMEM] * 6,
+        [((length, width), F32), ((length, width), BF16), ((length, width), BF16)],
+        [VMEM] * 4,
         (),
         5 * head_flops,
-        20 * length * width,
-    )(pinned(queries), pinned(keys), pinned(values), decay_t, gain_row, pinned(out_gate))
+        16 * length * width,
+    )(pinned(queries), pinned(keys), pinned(values), decay_t)
 
     gates, ups, downs = {}, {}, {}
 
@@ -552,7 +555,13 @@
     while 2 * step < spots:
         window = pack(block + block_decay * carry, block_decay * between)
         if step == 1:
-            window = after_all(window, moe_row)
+            gain_row = after_all(attn_gain, window).reshape(1, width)
+            moe_row = after_all(moe_gain, window).reshape(1, width)
+            gate = call(gate_kernel, [((length, width), F32)], [VMEM] * 2, (), 0, 6 * length * width)(
+                gain_row, pinned(out_gate)
+            )
+        if step == 2:
+            window = after_all(window, gate, moe_row)
         got, got_decay = unpack(lax.ppermute(window, "seq", shift(spots, 2 * step)), half)
         carry, between = carry + between * got, between * got_decay
         step *= 2
@@ -600,13 +609,8 @@
         size = sizes[g]
         outs, inputs, jobs = [], [], []
         for c, home in parts_of:
-            extra, piece = c == 0, pieces[c]
-            outs.append(((size + PAD * extra, (2 if home else 4) * piece), BF16))
-            if home:
-                outs.append(((size, 2 * piece), F32))
-                inputs.append(state["came", g, c])
-                if extra:
-                    outs.append(((PAD, LANES), F32))
+            extra = c == 0 and not home
+            outs.append(((size + PAD * extra, 4 * pieces[c]), F32 if home else BF16))
             inputs += [gates[c], ups[c]]
             jobs.append((home, extra))
         made = call(
@@ -619,15 +623,27 @@
         )(part, next_turn(state["rows", g]), state["squares", g], *inputs)
         made = [made] if len(outs) == 1 else list(made)
         turn.append(made[0])
-        for (c, home), (_, extra) in zip(parts_of, jobs):
-            cross = made.pop(0)
+        for (c, home), sums in zip(parts_of, made):
             if home:
-                state["stay", g, c] = made.pop(0)
-                if extra:
-                    state["lines", g] = made.pop(0)
-                state["seen", g, c] = lax.ppermute(cross, "head", flip(parts, 2))
+                state["home", g, c] = sums
             else:
-                state["came", g, c] = lax.ppermute(cross, "head", flip(parts, 1))
+                state["came", g, c] = lax.ppermute(sums, "head", flip(parts, 1))
+
+    def add(g, c):
+        size, piece, extra = sizes[g], pieces[c], c == 0
+        cross, state["stay", g, c], *lines = call(
+            functools.partial(add_kernel, extra),
+            [((size + PAD * extra, 2 * piece), BF16), ((size, 2 * piece), F32)]
+            + [((PAD, LANES), F32)] * extra,
+            [VMEM] * 3,
+            (),
+            0,
+            32 * size * piece,
+        )(next_turn(state["home", g, c]), state["came", g, c], state["squares", g])
+        if extra:
+            state["lines", g] = lines[0]
+        state["seen", g, c] = lax.ppermute(cross, "head", flip(parts, 2))
+        turn.append(cross)
 
     def act(g, c):
         size, piece, extra = sizes[g], pieces[c], c == 0
@@ -669,12 +685,12 @@
             for k, block in zip(GROUPS[g], out):
                 returned[k] = exchange(block, k)
 
-    def late_fetch():
-        turn.append(fetch(FETCH, turn[-1]))
+    def late_fetch(n):
+        turn.append(fetch(FETCHES[n], turn[-1]))
 
     returned = {}
     for job, *where in PLAN:
-        {"gather": gather, "up": up, "act": act, "down": down, "fetch": late_fetch}[job](*where)
+        {"gather": gather, "up": up, "add": add, "act": act, "down": down, "fetch": late_fetch}[job](*where)
     stats = lax.psum(next_turn(stats), "head")
     return call(
         functools.partial(combine_kernel, float(width * parts)),
@@ -687,13 +703,17 @@
 
 
 PLAN = (
-    ("fetch",),
+    ("fetch", 0),
     ("gather", 0),
     ("up", 0, (0, False)),
     ("up", 0, (0, True), (1, False)),
+    ("add", 0, 0),
     ("up", 0, (1, True), (2, False)),
+    ("add", 0, 1),
+    ("fetch", 1),
+    ("act", 0, 0),
     ("up", 0, (2, True)),
-    ("act", 0, 0),
+    ("add", 0, 2),
     ("act", 0, 1),
     ("act", 0, 2),
     ("down", 0, 0),

time: 173 us -> 160 us (0.925)
  waiting for transfers between devices: 77.3 us -> 66.1 us
  local copies, waits for them, and re-layouts: 4.86 us -> 1.56 us
    ppermute x6, waiting for transfers between devices: 32.1 us -> 18.4 us  [the longest x3 18.4 us: add(): state['seen', g, c] = lax.ppermute(cross, 'head', flip(parts, 2))]
    ppermute x14, waiting for transfers between devices: 14.5 us -> 20 us  [exchange(): return lax.ppermute(block, 'seq', flip(spots, k)) if k else block]
    unnamed x16 -> x8, local copies, waits for them, and re-layouts: 3.36 us -> 1.42 us
    pallas_call x0 -> x4, Pallas kernels: none -> 1.74 us  [the longest x1 1.21 us: local_fast(): call(gate_kernel, [((length, width), F32)], [VMEM] * 2, (), 0, 6 * length...]
    pallas_call x1 -> x2, Pallas kernels: 13.4 us -> 14.3 us  [fetch(): pl.pallas_call(functools.partial(fetch_kernel, jobs), out_shape=shapes, i...]
  transfers between devices with their start and end apart: 33 -> 33, of which waited for: 15 -> 17; matrix products, arithmetic and copies ran while one was open for 1% -> 0% of each run, Pallas kernels for 14% -> 21%
where the time goes in v2:
time: 160 us; the launch traced here: 159 us
  waiting for transfers between devices  66.1 us (41%)
  Pallas kernels  45.5 us (28%)
  starting transfers between devices  38.9 us (24%)
  blocking collectives  6.03 us (4%)
    ppermute x14, waiting for transfers between devices, exchange(): return lax.ppermute(block, 'seq', flip(spots, k)) if k else block  20 us
    ppermute x14, starting transfers between devices, exchange(): return lax.ppermute(block, 'seq', flip(spots, k)) if k else block  19.5 us
    ppermute x3, waiting for transfers between devices, add(): state['seen', g, c] = lax.ppermute(cross, 'head', flip(parts, 2))  18.4 us
    pallas_call x2, Pallas kernels, fetch(): pl.pallas_call(functools.partial(fetch_kernel, jobs), out_shape=shapes, i...  14.3 us
    ppermute x3, waiting for transfers between devices, act(): across = lax.ppermute(made, 'head', flip(parts, 2))  10.8 us
    ppermute x2, waiting for transfers between devices, local_fast(): lax.ppermute(window, 'seq', shift(spots, 2 * step))  10.5 us
    pallas_call x4, Pallas kernels, up(): call(functools.partial(up_kernel, jobs), outs, [SMEM] + [VMEM] * (2 + len...  10.2 us
    ppermute x2, starting transfers between devices, local_fast(): lax.ppermute(window, 'seq', shift(spots, 2 * step))  8.16 us
  transfers between devices with their start and end apart: 33, of which 17 were waited for; matrix products, arithmetic and copies ran while one was open for 0% of the time, Pallas kernels for 21%

profile of v2, /device:TPU:8, one launch (start us, length us, event | category | flops | bytes accessed | tf_op | source)
XLA Modules:
  0.0 159.2 jit_solution(10570831869499339696)
XLA Ops:
  5.3 4.4 %shard_map.127 = (f32[128,1536]{1,0:T(8,128)S(1)}, bf16[128,1536]{1,0:T(8,128)(2,1)S(1)}, bf16[128,1536]{1,0:T(8,128)(2,1)S(1)}) custom-call(bf16[128,1536]{1,0:T(8,128)(2,1)} %queries_ref.1, bf16[128,1536]{1,0:T(8,128)(2,1)} %keys_ref.3, bf16[128,1536]{1,0:T(8,128)(2,1)} %values_ref.3, f32[12,128]{1,0:T(8,128)S(1)} %bitcast.15), custom_call_target="tpu_custom_call" | custom-call | flops 251658240 | bytes 3145728 | tf_op jit(solution)/shard_map/pallas_call | solution.py:512
  10.1 3.5 %collective-permute-start.1 = (bf16[784,128]{1,0:T(8,128)(2,1)S(1)}, bf16[784,128]{1,0:T(8,128)(2,1)S(1)}, u32[]{:S(2)}, u32[]{:S(2)}) collective-permute-start(bf16[784,128]{1,0:T(8,128)(2,1)S(1)} %maximum_maximum_fusion), channel_id=1, source_target_pairs={{0,8},{4,12},{8,16},{12,20},{16,24},{20,28},{1,9},{5,13},{9,17},{1... | collective-permute-start | bytes 602120 | tf_op jit(solution)/shard_map/ppermute | solution.py:565
  14.9 3.5 %collective-permute-done.1 = bf16[784,128]{1,0:T(8,128)(2,1)S(1)} collective-permute-done((bf16[784,128]{1,0:T(8,128)(2,1)S(1)}, bf16[784,128]{1,0:T(8,128)(2,1)S(1)}, u32[]{:S(2)}, u32[]{:S(2)}) %collective-permute-start.1) | collective-permute-done | bytes 200736 | tf_op jit(solution)/shard_map/ppermute | solution.py:565
  18.7 4.7 %collective-permute-start.2 = (bf16[784,128]{1,0:T(8,128)(2,1)S(1)}, bf16[784,128]{1,0:T(8,128)(2,1)S(1)}, u32[]{:S(2)}, u32[]{:S(2)}) collective-permute-start(bf16[784,128]{1,0:T(8,128)(2,1)S(1)} %maximum_maximum_fusion.1), channel_id=1, source_target_pairs={{0,16},{4,20},{8,24},{12,28},{1,17},{5,21},{9,25},{13,29},{2,18},{... | collective-permute-start | bytes 602120 | tf_op jit(solution)/shard_map/ppermute | solution.py:565
  23.4 7.0 %collective-permute-done.2 = bf16[784,128]{1,0:T(8,128)(2,1)S(1)} collective-permute-done((bf16[784,128]{1,0:T(8,128)(2,1)S(1)}, bf16[784,128]{1,0:T(8,128)(2,1)S(1)}, u32[]{:S(2)}, u32[]{:S(2)}) %collective-permute-start.2) | collective-permute-done | bytes 200736 | tf_op jit(solution)/shard_map/ppermute | solution.py:565
  31.2 6.2 %collective-permute-done.3.other_ref = bf16[768,128]{1,0:T(8,128)(2,1)S(1)} collective-permute-done((bf16[768,128]{1,0:T(8,128)(2,1)S(1)}, bf16[768,128]{1,0:T(8,128)(2,1)S(1)}, u32[]{:S(2)}, u32[]{:S(2)}) %collective-permute-start.3) | collective-permute-done | bytes 196640 | tf_op jit(solution)/shard_map/ppermute | solution.py:571
  40.2 3.2 %collective-permute-start.6 = (bf16[36,1536]{1,0:T(8,128)(2,1)S(1)}, bf16[36,1536]{1,0:T(8,128)(2,1)S(1)}, u32[]{:S(2)}, u32[]{:S(2)}) collective-permute-start(bf16[36,1536]{1,0:T(8,128)(2,1)S(1)} %get-tuple-element.95), channel_id=1, source_target_pairs={{0,12},{4,8},{8,4},{12,0},{16,28},{20,24},{24,20},{28,16},{1,13},{... | collective-permute-start | bytes 331784 | tf_op jit(solution)/shard_map/ppermute | solution.py:585
  43.4 3.4 %collective-permute-start.7 = (bf16[36,1536]{1,0:T(8,128)(2,1)S(1)}, bf16[36,1536]{1,0:T(8,128)(2,1)S(1)}, u32[]{:S(2)}, u32[]{:S(2)}) collective-permute-start(bf16[36,1536]{1,0:T(8,128)(2,1)S(1)} %get-tuple-element.96), channel_id=1, source_target_pairs={{0,16},{4,20},{8,24},{12,28},{16,0},{20,4},{24,8},{28,12},{1,17},{... | collective-permute-start | bytes 331784 | tf_op jit(solution)/shard_map/ppermute | solution.py:585
  49.8 9.2 %shard_map.131 = (bf16[1536,1024]{1,0:T(8,128)(2,1)S(1)}, bf16[1536,2048]{1,0:T(8,128)(2,1)S(1)}, bf16[1536,1536]{1,0:T(8,128)(2,1)S(1)}, bf16[1536,1024]{1,0:T(...) custom-call(bf16[1536,4608]{1,0:T(8,128)(2,1)} %gate_ref.3, bf16[1536,4608]{1,0:T(8,128)(2,1)} %up_ref.1, ...), custom_call_target="tpu_custom_call" | custom-call | bytes 1048576 | tf_op jit(solution)/shard_map/pallas_call | solution.py:530
  59.2 2.6 %collective-permute-done.8.rest_5_ = bf16[36,1536]{1,0:T(8,128)(2,1)S(1)} collective-permute-done((bf16[36,1536]{1,0:T(8,128)(2,1)S(1)}, bf16[36,1536]{1,0:T(8,128)(2,1)S(1)}, u32[]{:S(2)}, u32[]{:S(2)}) %collective-permute-start.8) | collective-permute-done | bytes 110624 | tf_op jit(solution)/shard_map/ppermute | solution.py:585
  61.8 3.3 %collective-permute-done.9.rest_6_ = bf16[36,1536]{1,0:T(8,128)(2,1)S(1)} collective-permute-done((bf16[36,1536]{1,0:T(8,128)(2,1)S(1)}, bf16[36,1536]{1,0:T(8,128)(2,1)S(1)}, u32[]{:S(2)}, u32[]{:S(2)}) %collective-permute-start.9) | collective-permute-done | bytes 110624 | tf_op jit(solution)/shard_map/ppermute | solution.py:585
  68.5 3.1 %shard_map.134 = (f32[288,1024]{1,0:T(8,128)S(1)}, bf16[288,2048]{1,0:T(8,128)(2,1)S(1)}) custom-call(s32[1]{0:T(128)} %bitcast.12.place_ref, bf16[288,1536]{1,0:T(8,128)(2,1)S(1)} %get-tuple-element.123.rows_ref, bf16[16,128]{1,0:T(8,128)(2,1)S(1)} %get-tuple-element.102.squares_ref, bf16[1536,1024]{1,0:T(8,128)(2,1)S(1)} %get-tuple-element.90.refs_0_, ...), custom_call_target="tpu_custom_call" | custom-call | flops 2717908992 | bytes 3538944 | tf_op jit(solution)/shard_map/pallas_call | solution.py:616
  72.3 3.9 %shard_map.136 = (f32[288,2048]{1,0:T(8,128)S(1)}, bf16[288,1536]{1,0:T(8,128)(2,1)S(1)}) custom-call(s32[1]{0:T(128)} %bitcast.12.place_ref, bf16[288,1536]{1,0:T(8,128)(2,1)S(1)} %get-tuple-element.123.rows_ref, bf16[16,128]{1,0:T(8,128)(2,1)S(1)} %get-tuple-element.102.squares_ref, bf16[1536,2048]{1,0:T(8,128)(2,1)S(1)} %get-tuple-element.105.refs_2_.refs_0_, ...), custom_call_target="tpu_custom_call" | custom-call | flops 3170893824 | bytes 3538944 | tf_op jit(solution)/shard_map/pallas_call | solution.py:616
  78.6 5.1 %shard_map.138 = (bf16[1024,1536]{1,0:T(8,128)(2,1)S(1)}, bf16[2048,1536]{1,0:T(8,128)(2,1)S(1)}, bf16[1536,1536]{1,0:T(8,128)(2,1)S(1)}) custom-call(bf16[1536,4608]{1,0:T(8,128)(2,1)} %gate_ref.3, bf16[1536,4608]{1,0:T(8,128)(2,1)} %up_ref.1, bf16[4608,1536]{1,0:T(8,128)(2,1)} %down_ref.1), custom_call_target="tpu_custom_call" | custom-call | bytes 1048576 | tf_op jit(solution)/shard_map/pallas_call | solution.py:530
  83.8 2.8 %collective-permute-done.13.seen_ref = bf16[304,512]{1,0:T(8,128)(2,1)S(1)} collective-permute-done((bf16[304,512]{1,0:T(8,128)(2,1)S(1)}, bf16[304,512]{1,0:T(8,128)(2,1)S(1)}, u32[]{:S(2)}, u32[]{:S(2)}) %collective-permute-start.13) | collective-permute-done | bytes 311328 | tf_op jit(solution)/shard_map/ppermute | solution.py:645
  90.7 8.5 %collective-permute-done.15.seen_ref = bf16[288,1024]{1,0:T(8,128)(2,1)S(1)} collective-permute-done((bf16[288,1024]{1,0:T(8,128)(2,1)S(1)}, bf16[288,1024]{1,0:T(8,128)(2,1)S(1)}, u32[]{:S(2)}, u32[]{:S(2)}) %collective-permute-start.15) | collective-permute-done | bytes 589856 | tf_op jit(solution)/shard_map/ppermute | solution.py:645
  101.6 7.1 %collective-permute-done.16.seen_ref = bf16[288,768]{1,0:T(8,128)(2,1)S(1)} collective-permute-done((bf16[288,768]{1,0:T(8,128)(2,1)S(1)}, bf16[288,768]{1,0:T(8,128)(2,1)S(1)}, u32[]{:S(2)}, u32[]{:S(2)}) %collective-permute-start.16) | collective-permute-done | bytes 442400 | tf_op jit(solution)/shard_map/ppermute | solution.py:645
  110.6 4.5 %collective-permute-done.20.rest_1_ = bf16[288,512]{1,0:T(8,128)(2,1)S(1)} collective-permute-done((bf16[288,512]{1,0:T(8,128)(2,1)S(1)}, bf16[288,512]{1,0:T(8,128)(2,1)S(1)}, u32[]{:S(2)}, u32[]{:S(2)}) %collective-permute-start.20) | collective-permute-done | bytes 294944 | tf_op jit(solution)/shard_map/ppermute | solution.py:664
  115.5 2.6 %collective-permute-done.17.rest_1_ = bf16[288,256]{1,0:T(8,128)(2,1)S(1)} collective-permute-done((bf16[288,256]{1,0:T(8,128)(2,1)S(1)}, bf16[288,256]{1,0:T(8,128)(2,1)S(1)}, u32[]{:S(2)}, u32[]{:S(2)}) %collective-permute-start.17) | collective-permute-done | bytes 147488 | tf_op jit(solution)/shard_map/ppermute | solution.py:664
  118.7 3.7 %collective-permute-done.23.rest_1_ = bf16[288,384]{1,0:T(8,128)(2,1)S(1)} collective-permute-done((bf16[288,384]{1,0:T(8,128)(2,1)S(1)}, bf16[288,384]{1,0:T(8,128)(2,1)S(1)}, u32[]{:S(2)}, u32[]{:S(2)}) %collective-permute-start.23) | collective-permute-done | bytes 221216 | tf_op jit(solution)/shard_map/ppermute | solution.py:664
  137.3 6.0 %psum.7.stats_ref = f32[16,128]{1,0:T(8,128)S(1)} all-reduce(f32[16,128]{1,0:T(8,128)S(1)} %get-tuple-element.137), channel_id=1, replica_groups=mesh['seq'=8,'head'=4] {'head'}, use_global_device_ids=true, to_apply=%region_0.1 | all-reduce | flops 2048 | bytes 16384 | tf_op jit(solution)/shard_map/psum | solution.py:694
  143.4 6.0 %collective-permute-done.30.rest_5_ = bf16[36,1536]{1,0:T(8,128)(2,1)S(1)} collective-permute-done((bf16[36,1536]{1,0:T(8,128)(2,1)S(1)}, bf16[36,1536]{1,0:T(8,128)(2,1)S(1)}, u32[]{:S(2)}, u32[]{:S(2)}) %collective-permute-start.30) | collective-permute-done | bytes 110624 | tf_op jit(solution)/shard_map/ppermute | solution.py:585
  149.4 4.7 %collective-permute-done.31.rest_6_ = bf16[36,1536]{1,0:T(8,128)(2,1)S(1)} collective-permute-done((bf16[36,1536]{1,0:T(8,128)(2,1)S(1)}, bf16[36,1536]{1,0:T(8,128)(2,1)S(1)}, u32[]{:S(2)}, u32[]{:S(2)}) %collective-permute-start.31) | collective-permute-done | bytes 110624 | tf_op jit(solution)/shard_map/ppermute | solution.py:585
  155.8 3.4 %shard_map.147 = bf16[128,1536]{1,0:T(8,128)(2,1)} custom-call(s32[1]{0:T(128)} %bitcast.place_ref, bf16[128,1536]{1,0:T(8,128)(2,1)S(1)} %get-tuple-element.85.hidden_ref, f32[16,128]{1,0:T(8,128)S(1)} %psum.7.stats_ref, s32[2,128]{1,0:T(2,128)} %bitcast.27, bf16[36,1536]{1,0:T(8,128)(2,1)S(1)} %get-tuple-element.136.rest_0_, ...), custom_call_target="tpu_custom_call" | custom-call | flops 226492416 | bytes 1572864 | tf_op jit(solution)/shard_map/pallas_call | solution.py:695
  (90 shorter events, 46.2 us)
Async XLA Ops:
  10.1 8.3 %collective-permute-start.1 = (bf16[784,128]{1,0:T(8,128)(2,1)S(1)}, bf16[784,128]{1,0:T(8,128)(2,1)S(1)}, u32[]{:S(2)}, u32[]{:S(2)}) collective-permute-start(bf16[784,128]{1,0:T(8,128)(2,1)S(1)} %maximum_maximum_fusion), channel_id=1, source_target_pairs={{0,8},{4,12},{8,16},{12,20},{16,24},{20,28},{1,9},{5,13},{9,17},{1... | collective-permute-start | bytes 602120 | tf_op jit(solution)/shard_map/ppermute | solution.py:565
  18.7 11.7 %collective-permute-start.2 = (bf16[784,128]{1,0:T(8,128)(2,1)S(1)}, bf16[784,128]{1,0:T(8,128)(2,1)S(1)}, u32[]{:S(2)}, u32[]{:S(2)}) collective-permute-start(bf16[784,128]{1,0:T(8,128)(2,1)S(1)} %maximum_maximum_fusion.1), channel_id=1, source_target_pairs={{0,16},{4,20},{8,24},{12,28},{1,17},{5,21},{9,25},{13,29},{2,18},{... | collective-permute-start | bytes 602120 | tf_op jit(solution)/shard_map/ppermute | solution.py:565
  40.2 8.1 %collective-permute-start.5 = (bf16[36,1536]{1,0:T(8,128)(2,1)S(1)}, bf16[36,1536]{1,0:T(8,128)(2,1)S(1)}, u32[]{:S(2)}, u32[]{:S(2)}) collective-permute-start(bf16[36,1536]{1,0:T(8,128)(2,1)S(1)} %get-tuple-element.94), channel_id=1, source_target_pairs={{0,8},{4,12},{8,0},{12,4},{16,24},{20,28},{24,16},{28,20},{1,9},{5... | collective-permute-start | bytes 331784 | tf_op jit(solution)/shard_map/ppermute | solution.py:585
  40.2 18.8 %collective-permute-start.6 = (bf16[36,1536]{1,0:T(8,128)(2,1)S(1)}, bf16[36,1536]{1,0:T(8,128)(2,1)S(1)}, u32[]{:S(2)}, u32[]{:S(2)}) collective-permute-start(bf16[36,1536]{1,0:T(8,128)(2,1)S(1)} %get-tuple-element.95), channel_id=1, source_target_pairs={{0,12},{4,8},{8,4},{12,0},{16,28},{20,24},{24,20},{28,16},{1,13},{... | collective-permute-start | bytes 331784 | tf_op jit(solution)/shard_map/ppermute | solution.py:585
  43.4 15.8 %collective-permute-start.7 = (bf16[36,1536]{1,0:T(8,128)(2,1)S(1)}, bf16[36,1536]{1,0:T(8,128)(2,1)S(1)}, u32[]{:S(2)}, u32[]{:S(2)}) collective-permute-start(bf16[36,1536]{1,0:T(8,128)(2,1)S(1)} %get-tuple-element.96), channel_id=1, source_target_pairs={{0,16},{4,20},{8,24},{12,28},{16,0},{20,4},{24,8},{28,12},{1,17},{... | collective-permute-start | bytes 331784 | tf_op jit(solution)/shard_map/ppermute | solution.py:585
  46.8 15.0 %collective-permute-start.8 = (bf16[36,1536]{1,0:T(8,128)(2,1)S(1)}, bf16[36,1536]{1,0:T(8,128)(2,1)S(1)}, u32[]{:S(2)}, u32[]{:S(2)}) collective-permute-start(bf16[36,1536]{1,0:T(8,128)(2,1)S(1)} %get-tuple-element.97), channel_id=1, source_target_pairs={{0,20},{4,16},{8,28},{12,24},{16,4},{20,0},{24,12},{28,8},{1,21},{... | collective-permute-start | bytes 331784 | tf_op jit(solution)/shard_map/ppermute | solution.py:585
  46.8 18.3 %collective-permute-start.9 = (bf16[36,1536]{1,0:T(8,128)(2,1)S(1)}, bf16[36,1536]{1,0:T(8,128)(2,1)S(1)}, u32[]{:S(2)}, u32[]{:S(2)}) collective-permute-start(bf16[36,1536]{1,0:T(8,128)(2,1)S(1)} %get-tuple-element.98), channel_id=1, source_target_pairs={{0,24},{4,28},{8,16},{12,20},{16,8},{20,12},{24,0},{28,4},{1,25},{... | collective-permute-start | bytes 331784 | tf_op jit(solution)/shard_map/ppermute | solution.py:585
  48.3 18.4 %collective-permute-start.10 = (bf16[36,1536]{1,0:T(8,128)(2,1)S(1)}, bf16[36,1536]{1,0:T(8,128)(2,1)S(1)}, u32[]{:S(2)}, u32[]{:S(2)}) collective-permute-start(bf16[36,1536]{1,0:T(8,128)(2,1)S(1)} %get-tuple-element.99), channel_id=1, source_target_pairs={{0,28},{4,24},{8,20},{12,16},{16,12},{20,8},{24,4},{28,0},{1,29},{... | collective-permute-start | bytes 331784 | tf_op jit(solution)/shard_map/ppermute | solution.py:585
  76.2 12.7 %collective-permute-start.14 = (bf16[288,1536]{1,0:T(8,128)(2,1)S(1)}, bf16[288,1536]{1,0:T(8,128)(2,1)S(1)}, u32[]{:S(2)}, u32[]{:S(2)}) collective-permute-start(bf16[288,1536]{1,0:T(8,128)(2,1)S(1)} %get-tuple-element.124), channel_id=1, source_target_pairs={{0,1},{1,0},{2,3},{3,2},{4,5},{5,4},{6,7},{7,6},{8,9},{9,8},{10,11... | collective-permute-start | bytes 2654216 | tf_op jit(solution)/shard_map/ppermute | solution.py:630
  76.3 10.3 %collective-permute-start.13 = (bf16[304,512]{1,0:T(8,128)(2,1)S(1)}, bf16[304,512]{1,0:T(8,128)(2,1)S(1)}, u32[]{:S(2)}, u32[]{:S(2)}) collective-permute-start(bf16[304,512]{1,0:T(8,128)(2,1)S(1)} %get-tuple-element.109), channel_id=1, source_target_pairs={{0,2},{1,3},{2,0},{3,1},{4,6},{5,7},{6,4},{7,5},{8,10},{9,11},{10,... | collective-permute-start | bytes 933896 | tf_op jit(solution)/shard_map/ppermute | solution.py:645
  78.1 21.2 %collective-permute-start.15 = (bf16[288,1024]{1,0:T(8,128)(2,1)S(1)}, bf16[288,1024]{1,0:T(8,128)(2,1)S(1)}, u32[]{:S(2)}, u32[]{:S(2)}) collective-permute-start(bf16[288,1024]{1,0:T(8,128)(2,1)S(1)} %get-tuple-element.115), channel_id=1, source_target_pairs={{0,2},{1,3},{2,0},{3,1},{4,6},{5,7},{6,4},{7,5},{8,10},{9,11},{10,... | collective-permute-start | bytes 1769480 | tf_op jit(solution)/shard_map/ppermute | solution.py:645
  89.1 19.6 %collective-permute-start.16 = (bf16[288,768]{1,0:T(8,128)(2,1)S(1)}, bf16[288,768]{1,0:T(8,128)(2,1)S(1)}, u32[]{:S(2)}, u32[]{:S(2)}) collective-permute-start(bf16[288,768]{1,0:T(8,128)(2,1)S(1)} %get-tuple-element.127), channel_id=1, source_target_pairs={{0,2},{1,3},{2,0},{3,1},{4,6},{5,7},{6,4},{7,5},{8,10},{9,11},{10,... | collective-permute-start | bytes 1327112 | tf_op jit(solution)/shard_map/ppermute | solution.py:645
  99.5 15.5 %collective-permute-start.20 = (bf16[288,512]{1,0:T(8,128)(2,1)S(1)}, bf16[288,512]{1,0:T(8,128)(2,1)S(1)}, u32[]{:S(2)}, u32[]{:S(2)}) collective-permute-start(bf16[288,512]{1,0:T(8,128)(2,1)S(1)} %shard_map.142.rest_0_), channel_id=1, source_target_pairs={{0,2},{1,3},{2,0},{3,1},{4,6},{5,7},{6,4},{7,5},{8,10},{9,11},{10,... | collective-permute-start | bytes 884744 | tf_op jit(solution)/shard_map/ppermute | solution.py:664
  101.1 17.1 %collective-permute-start.17 = (bf16[288,256]{1,0:T(8,128)(2,1)S(1)}, bf16[288,256]{1,0:T(8,128)(2,1)S(1)}, u32[]{:S(2)}, u32[]{:S(2)}) collective-permute-start(bf16[288,256]{1,0:T(8,128)(2,1)S(1)} %get-tuple-element.131.rest_0_), channel_id=1, source_target_pairs={{0,2},{1,3},{2,0},{3,1},{4,6},{5,7},{6,4},{7,5},{8,10},{9,11},{10,... | collective-permute-start | bytes 442376 | tf_op jit(solution)/shard_map/ppermute | solution.py:664
  109.0 13.4 %collective-permute-start.23 = (bf16[288,384]{1,0:T(8,128)(2,1)S(1)}, bf16[288,384]{1,0:T(8,128)(2,1)S(1)}, u32[]{:S(2)}, u32[]{:S(2)}) collective-permute-start(bf16[288,384]{1,0:T(8,128)(2,1)S(1)} %shard_map.143.rest_0_), channel_id=1, source_target_pairs={{0,2},{1,3},{2,0},{3,1},{4,6},{5,7},{6,4},{7,5},{8,10},{9,11},{10,... | collective-permute-start | bytes 663560 | tf_op jit(solution)/shard_map/ppermute | solution.py:664
  110.5 13.2 %collective-permute-start.21 = (bf16[288,512]{1,0:T(8,128)(2,1)S(1)}, bf16[288,512]{1,0:T(8,128)(2,1)S(1)}, u32[]{:S(2)}, u32[]{:S(2)}) collective-permute-start(bf16[288,512]{1,0:T(8,128)(2,1)S(1)} %shard_map.142.rest_0_), channel_id=1, source_target_pairs={{0,1},{1,0},{2,3},{3,2},{4,5},{5,4},{6,7},{7,6},{8,9},{9,8},{10,11... | collective-permute-start | bytes 884744 | tf_op jit(solution)/shard_map/ppermute | solution.py:665
  115.0 8.7 %collective-permute-start.22 = (bf16[288,512]{1,0:T(8,128)(2,1)S(1)}, bf16[288,512]{1,0:T(8,128)(2,1)S(1)}, u32[]{:S(2)}, u32[]{:S(2)}) collective-permute-start(bf16[288,512]{1,0:T(8,128)(2,1)S(1)} %collective-permute-done.20.rest_1_), channel_id=1, source_target_pairs={{0,1},{1,0},{2,3},{3,2},{4,5},{5,4},{6,7},{7,6},{8,9},{9,8},{10,11... | collective-permute-start | bytes 884744 | tf_op jit(solution)/shard_map/ppermute | solution.py:672
  118.2 7.5 %collective-permute-start.24 = (bf16[288,384]{1,0:T(8,128)(2,1)S(1)}, bf16[288,384]{1,0:T(8,128)(2,1)S(1)}, u32[]{:S(2)}, u32[]{:S(2)}) collective-permute-start(bf16[288,384]{1,0:T(8,128)(2,1)S(1)} %shard_map.143.rest_0_), channel_id=1, source_target_pairs={{0,1},{1,0},{2,3},{3,2},{4,5},{5,4},{6,7},{7,6},{8,9},{9,8},{10,11... | collective-permute-start | bytes 663560 | tf_op jit(solution)/shard_map/ppermute | solution.py:665
  129.3 7.8 %collective-permute-start.27 = (bf16[36,1536]{1,0:T(8,128)(2,1)S(1)}, bf16[36,1536]{1,0:T(8,128)(2,1)S(1)}, u32[]{:S(2)}, u32[]{:S(2)}) collective-permute-start(bf16[36,1536]{1,0:T(8,128)(2,1)S(1)} %get-tuple-element.139), channel_id=1, source_target_pairs={{0,8},{4,12},{8,0},{12,4},{16,24},{20,28},{24,16},{28,20},{1,9},{5... | collective-permute-start | bytes 331784 | tf_op jit(solution)/shard_map/ppermute | solution.py:585
  129.3 14.0 %collective-permute-start.28 = (bf16[36,1536]{1,0:T(8,128)(2,1)S(1)}, bf16[36,1536]{1,0:T(8,128)(2,1)S(1)}, u32[]{:S(2)}, u32[]{:S(2)}) collective-permute-start(bf16[36,1536]{1,0:T(8,128)(2,1)S(1)} %get-tuple-element.140), channel_id=1, source_target_pairs={{0,12},{4,8},{8,4},{12,0},{16,28},{20,24},{24,20},{28,16},{1,13},{... | collective-permute-start | bytes 331784 | tf_op jit(solution)/shard_map/ppermute | solution.py:585
  131.3 12.0 %collective-permute-start.29 = (bf16[36,1536]{1,0:T(8,128)(2,1)S(1)}, bf16[36,1536]{1,0:T(8,128)(2,1)S(1)}, u32[]{:S(2)}, u32[]{:S(2)}) collective-permute-start(bf16[36,1536]{1,0:T(8,128)(2,1)S(1)} %get-tuple-element.141), channel_id=1, source_target_pairs={{0,16},{4,20},{8,24},{12,28},{16,0},{20,4},{24,8},{28,12},{1,17},{... | collective-permute-start | bytes 331784 | tf_op jit(solution)/shard_map/ppermute | solution.py:585
  132.7 16.7 %collective-permute-start.30 = (bf16[36,1536]{1,0:T(8,128)(2,1)S(1)}, bf16[36,1536]{1,0:T(8,128)(2,1)S(1)}, u32[]{:S(2)}, u32[]{:S(2)}) collective-permute-start(bf16[36,1536]{1,0:T(8,128)(2,1)S(1)} %get-tuple-element.142), channel_id=1, source_target_pairs={{0,20},{4,16},{8,28},{12,24},{16,4},{20,0},{24,12},{28,8},{1,21},{... | collective-permute-start | bytes 331784 | tf_op jit(solution)/shard_map/ppermute | solution.py:585
  135.2 18.9 %collective-permute-start.31 = (bf16[36,1536]{1,0:T(8,128)(2,1)S(1)}, bf16[36,1536]{1,0:T(8,128)(2,1)S(1)}, u32[]{:S(2)}, u32[]{:S(2)}) collective-permute-start(bf16[36,1536]{1,0:T(8,128)(2,1)S(1)} %get-tuple-element.143), channel_id=1, source_target_pairs={{0,24},{4,28},{8,16},{12,20},{16,8},{20,12},{24,0},{28,4},{1,25},{... | collective-permute-start | bytes 331784 | tf_op jit(solution)/shard_map/ppermute | solution.py:585
  137.1 18.7 %collective-permute-start.32 = (bf16[36,1536]{1,0:T(8,128)(2,1)S(1)}, bf16[36,1536]{1,0:T(8,128)(2,1)S(1)}, u32[]{:S(2)}, u32[]{:S(2)}) collective-permute-start(bf16[36,1536]{1,0:T(8,128)(2,1)S(1)} %get-tuple-element.144), channel_id=1, source_target_pairs={{0,28},{4,24},{8,20},{12,16},{16,12},{20,8},{24,4},{28,0},{1,29},{... | collective-permute-start | bytes 331784 | tf_op jit(solution)/shard_map/ppermute | solution.py:585
  (13 other events, 77.3 us)

commit v3 on v2

--- a/solution.py
+++ b/solution.py
@@ -411,10 +411,8 @@
             out_ref[...] = total[s * capacity : (s + 1) * capacity].astype(BF16)
 
 
-def combine_kernel(full_width, place_ref, hidden_ref, stats_ref, routes_ref, *rest):
-    returned_refs, (out_ref, rank_ref, weight_ref) = rest[:-3], rest[-3:]
-    count, slots = len(returned_refs), returned_refs[0].shape[0]
-    length = hidden_ref.shape[0]
+def weights_kernel(full_width, place_ref, stats_ref, routes_ref, high_ref, low_ref, rank_ref, weight_ref):
+    count, slots, length = high_ref.shape
     first, second, rank_ref[...] = expert_table(routes_ref, count)
     scale = lax.rsqrt(stats_ref[count : count + 1, :] / full_width + 1e-06)
     logits = stats_ref[0:count, :] * scale
@@ -423,12 +421,18 @@
     )
     weight_ref[...] = jnp.where(first, 1.0 / (1.0 + jnp.exp(-gap)), 1.0 / (1.0 + jnp.exp(gap)))
     slot = lax.broadcasted_iota(jnp.int32, (slots, length), 0)
-    total = hidden_ref[...].astype(F32)
-    for k, returned_ref in enumerate(returned_refs):
+    for k in range(count):
         line = pl.ds(place_ref[0] ^ k, 1)
         pick = jnp.where(rank_ref[line, :] == slot, weight_ref[line, :], 0.0)
-        high, low = split2(pick)
-        total = total + mm(high, returned_ref[...], TN) + mm(low, returned_ref[...], TN)
+        high_ref[k], low_ref[k] = split2(pick)
+
+
+def combine_kernel(order, high_ref, low_ref, hidden_ref, *rest):
+    returned_refs, out_ref = rest[:-1], rest[-1]
+    total = hidden_ref[...].astype(F32)
+    for k, returned_ref in zip(order, returned_refs):
+        rows = returned_ref[...]
+        total = total + mm(high_ref[k], rows, TN) + mm(low_ref[k], rows, TN)
     out_ref[...] = total.astype(BF16)
 
 
@@ -507,7 +511,7 @@
         [pltpu.VMEM((heads, LANES, LANES), F32), pltpu.VMEM((2, half, LANES), F32)],
         2 * head_flops,
         6 * length * width,
-    )(spot, pinned(keys), pinned(values), decay_t)
+    )(spot, pinned(keys), pinned(values), pinned(decay_t))
     own_decay = own_decay[:, None, :]
     inner, query_high, query_low = call(
         inner_kernel,
@@ -516,7 +520,7 @@
         (),
         5 * head_flops,
         16 * length * width,
-    )(pinned(queries), pinned(keys), pinned(values), decay_t)
+    )(pinned(queries), pinned(keys), pinned(values), pinned(decay_t))
 
     gates, ups, downs = {}, {}, {}
 
@@ -692,15 +696,26 @@
     for job, *where in PLAN:
         {"gather": gather, "up": up, "add": add, "act": act, "down": down, "fetch": late_fetch}[job](*where)
     stats = lax.psum(next_turn(stats), "head")
+    high, low = call(
+        functools.partial(weights_kernel, float(width * parts)),
+        [((spots, capacity, length), BF16)] * 2,
+        [SMEM] + [VMEM] * 2,
+        [pltpu.VMEM((count, length), jnp.int32), pltpu.VMEM((count, length), F32)],
+        0,
+        4 * spots * capacity * length,
+    )(spot, stats, pinned(routes_t))
+    order = RETURNS
     return call(
-        functools.partial(combine_kernel, float(width * parts)),
+        functools.partial(combine_kernel, order),
         [((length, width), BF16)],
-        [SMEM] + [VMEM] * (3 + spots),
-        [pltpu.VMEM((count, length), jnp.int32), pltpu.VMEM((count, length), F32)],
+        [VMEM] * (3 + spots),
+        (),
         4 * length * count * capacity * width,
         8 * length * width,
-    )(spot, hidden, stats, pinned(routes_t), *[returned[k] for k in range(spots)])
-
+    )(high, low, hidden, *[returned[k] for k in order])
+
+
+RETURNS = (0, 1, 2, 3, 4, 5, 6, 7)
 
 PLAN = (
     ("fetch", 0),

time: 160 us -> 156 us (0.975)
  waiting for transfers between devices: 66.1 us -> 63.1 us
  starting transfers between devices: 38.9 us -> 40.5 us
    ppermute x1, waiting for transfers between devices: 6.25 us -> 4.64 us  [local_fast(): other = lax.ppermute(other, 'seq', flip(spots, 1))]
    pallas_call x1 -> x2, Pallas kernels: 3.4 us -> 3.4 us  [the longest x1 2.55 us: local_fast(): call(functools.partial(combine_kernel, order), [((length, width), BF16)],...]
  transfers between devices with their start and end apart: 33 -> 33, of which waited for: 17 -> 17; matrix products, arithmetic and copies ran while one was open for 0% -> 0% of each run, Pallas kernels for 21% -> 22%
where the time goes in v3:
time: 156 us
  waiting for transfers between devices  63.1 us (40%)
  Pallas kernels  45.5 us (29%)
  starting transfers between devices  40.5 us (26%)
  blocking collectives  5.73 us (4%)
    ppermute x14, starting transfers between devices, exchange(): return lax.ppermute(block, 'seq', flip(spots, k)) if k else block  20.1 us
    ppermute x14, waiting for transfers between devices, exchange(): return lax.ppermute(block, 'seq', flip(spots, k)) if k else block  18.8 us
    ppermute x3, waiting for transfers between devices, add(): state['seen', g, c] = lax.ppermute(cross, 'head', flip(parts, 2))  18.5 us
    pallas_call x2, Pallas kernels, fetch(): pl.pallas_call(functools.partial(fetch_kernel, jobs), out_shape=shapes, i...  14.3 us
    ppermute x3, waiting for transfers between devices, act(): across = lax.ppermute(made, 'head', flip(parts, 2))  10.8 us
    pallas_call x4, Pallas kernels, up(): call(functools.partial(up_kernel, jobs), outs, [SMEM] + [VMEM] * (2 + len...  10.1 us
    ppermute x2, waiting for transfers between devices, local_fast(): lax.ppermute(window, 'seq', shift(spots, 2 * step))  9.52 us
    ppermute x2, starting transfers between devices, local_fast(): lax.ppermute(window, 'seq', shift(spots, 2 * step))  8.17 us
  transfers between devices with their start and end apart: 33, of which 17 were waited for; matrix products, arithmetic and copies ran while one was open for 0% of the time, Pallas kernels for 22%

profile of v3, /device:TPU:8, one launch (start us, length us, event | category | flops | bytes accessed | tf_op | source)
XLA Modules:
  0.0 156.0 jit_solution(17604694986484814795)
XLA Ops:
  3.9 4.4 %shard_map.127 = (f32[128,1536]{1,0:T(8,128)S(1)}, bf16[128,1536]{1,0:T(8,128)(2,1)S(1)}, bf16[128,1536]{1,0:T(8,128)(2,1)S(1)}) custom-call(bf16[128,1536]{1,0:T(8,128)(2,1)} %queries_ref.1, bf16[128,1536]{1,0:T(8,128)(2,1)} %keys_ref.3, bf16[128,1536]{1,0:T(8,128)(2,1)} %values_ref.3, f32[12,128]{1,0:T(8,128)} %bitcast.24), custom_call_target="tpu_custom_call" | custom-call | flops 251658240 | bytes 3145728 | tf_op jit(solution)/shard_map/pallas_call | solution.py:516
  9.4 3.5 %collective-permute-start.1 = (bf16[784,128]{1,0:T(8,128)(2,1)S(1)}, bf16[784,128]{1,0:T(8,128)(2,1)S(1)}, u32[]{:S(2)}, u32[]{:S(2)}) collective-permute-start(bf16[784,128]{1,0:T(8,128)(2,1)S(1)} %maximum_maximum_fusion), channel_id=1, source_target_pairs={{0,8},{4,12},{8,16},{12,20},{16,24},{20,28},{1,9},{5,13},{9,17},{1... | collective-permute-start | bytes 602120 | tf_op jit(solution)/shard_map/ppermute | solution.py:569
  14.2 3.0 %collective-permute-done.1 = bf16[784,128]{1,0:T(8,128)(2,1)S(1)} collective-permute-done((bf16[784,128]{1,0:T(8,128)(2,1)S(1)}, bf16[784,128]{1,0:T(8,128)(2,1)S(1)}, u32[]{:S(2)}, u32[]{:S(2)}) %collective-permute-start.1) | collective-permute-done | bytes 200736 | tf_op jit(solution)/shard_map/ppermute | solution.py:569
  17.5 4.7 %collective-permute-start.2 = (bf16[784,128]{1,0:T(8,128)(2,1)S(1)}, bf16[784,128]{1,0:T(8,128)(2,1)S(1)}, u32[]{:S(2)}, u32[]{:S(2)}) collective-permute-start(bf16[784,128]{1,0:T(8,128)(2,1)S(1)} %maximum_maximum_fusion.1), channel_id=1, source_target_pairs={{0,16},{4,20},{8,24},{12,28},{1,17},{5,21},{9,25},{13,29},{2,18},{... | collective-permute-start | bytes 602120 | tf_op jit(solution)/shard_map/ppermute | solution.py:569
  22.2 6.5 %collective-permute-done.2 = bf16[784,128]{1,0:T(8,128)(2,1)S(1)} collective-permute-done((bf16[784,128]{1,0:T(8,128)(2,1)S(1)}, bf16[784,128]{1,0:T(8,128)(2,1)S(1)}, u32[]{:S(2)}, u32[]{:S(2)}) %collective-permute-start.2) | collective-permute-done | bytes 200736 | tf_op jit(solution)/shard_map/ppermute | solution.py:569
  30.5 4.6 %collective-permute-done.3.other_ref = bf16[768,128]{1,0:T(8,128)(2,1)S(1)} collective-permute-done((bf16[768,128]{1,0:T(8,128)(2,1)S(1)}, bf16[768,128]{1,0:T(8,128)(2,1)S(1)}, u32[]{:S(2)}, u32[]{:S(2)}) %collective-permute-start.3) | collective-permute-done | bytes 196640 | tf_op jit(solution)/shard_map/ppermute | solution.py:575
  41.1 3.4 %collective-permute-start.7 = (bf16[36,1536]{1,0:T(8,128)(2,1)S(1)}, bf16[36,1536]{1,0:T(8,128)(2,1)S(1)}, u32[]{:S(2)}, u32[]{:S(2)}) collective-permute-start(bf16[36,1536]{1,0:T(8,128)(2,1)S(1)} %get-tuple-element.98), channel_id=1, source_target_pairs={{0,16},{4,20},{8,24},{12,28},{16,0},{20,4},{24,8},{28,12},{1,17},{... | collective-permute-start | bytes 331784 | tf_op jit(solution)/shard_map/ppermute | solution.py:589
  47.5 9.2 %shard_map.131 = (bf16[1536,1024]{1,0:T(8,128)(2,1)S(1)}, bf16[1536,2048]{1,0:T(8,128)(2,1)S(1)}, bf16[1536,1536]{1,0:T(8,128)(2,1)S(1)}, bf16[1536,1024]{1,0:T(...) custom-call(bf16[1536,4608]{1,0:T(8,128)(2,1)} %gate_ref.3, bf16[1536,4608]{1,0:T(8,128)(2,1)} %up_ref.1, ...), custom_call_target="tpu_custom_call" | custom-call | bytes 1048576 | tf_op jit(solution)/shard_map/pallas_call | solution.py:534
  56.9 2.6 %collective-permute-done.8.rest_5_ = bf16[36,1536]{1,0:T(8,128)(2,1)S(1)} collective-permute-done((bf16[36,1536]{1,0:T(8,128)(2,1)S(1)}, bf16[36,1536]{1,0:T(8,128)(2,1)S(1)}, u32[]{:S(2)}, u32[]{:S(2)}) %collective-permute-start.8) | collective-permute-done | bytes 110624 | tf_op jit(solution)/shard_map/ppermute | solution.py:589
  59.6 3.2 %collective-permute-done.9.rest_6_ = bf16[36,1536]{1,0:T(8,128)(2,1)S(1)} collective-permute-done((bf16[36,1536]{1,0:T(8,128)(2,1)S(1)}, bf16[36,1536]{1,0:T(8,128)(2,1)S(1)}, u32[]{:S(2)}, u32[]{:S(2)}) %collective-permute-start.9) | collective-permute-done | bytes 110624 | tf_op jit(solution)/shard_map/ppermute | solution.py:589
  66.8 3.1 %shard_map.134 = (f32[288,1024]{1,0:T(8,128)S(1)}, bf16[288,2048]{1,0:T(8,128)(2,1)S(1)}) custom-call(s32[1]{0:T(128)} %bitcast.12.place_ref, bf16[288,1536]{1,0:T(8,128)(2,1)S(1)} %get-tuple-element.125.rows_ref, bf16[16,128]{1,0:T(8,128)(2,1)S(1)} %get-tuple-element.104.squares_ref, bf16[1536,1024]{1,0:T(8,128)(2,1)S(1)} %get-tuple-element.92.refs_0_, ...), custom_call_target="tpu_custom_call" | custom-call | flops 2717908992 | bytes 3538944 | tf_op jit(solution)/shard_map/pallas_call | solution.py:620
  70.5 3.9 %shard_map.136 = (f32[288,2048]{1,0:T(8,128)S(1)}, bf16[288,1536]{1,0:T(8,128)(2,1)S(1)}) custom-call(s32[1]{0:T(128)} %bitcast.12.place_ref, bf16[288,1536]{1,0:T(8,128)(2,1)S(1)} %get-tuple-element.125.rows_ref, bf16[16,128]{1,0:T(8,128)(2,1)S(1)} %get-tuple-element.104.squares_ref, bf16[1536,2048]{1,0:T(8,128)(2,1)S(1)} %get-tuple-element.107.refs_2_.refs_0_, ...), custom_call_target="tpu_custom_call" | custom-call | flops 3170893824 | bytes 3538944 | tf_op jit(solution)/shard_map/pallas_call | solution.py:620
  76.9 5.1 %shard_map.138 = (bf16[1024,1536]{1,0:T(8,128)(2,1)S(1)}, bf16[2048,1536]{1,0:T(8,128)(2,1)S(1)}, bf16[1536,1536]{1,0:T(8,128)(2,1)S(1)}) custom-call(bf16[1536,4608]{1,0:T(8,128)(2,1)} %gate_ref.3, bf16[1536,4608]{1,0:T(8,128)(2,1)} %up_ref.1, bf16[4608,1536]{1,0:T(8,128)(2,1)} %down_ref.1), custom_call_target="tpu_custom_call" | custom-call | bytes 1048576 | tf_op jit(solution)/shard_map/pallas_call | solution.py:534
  82.0 2.8 %collective-permute-done.13.seen_ref = bf16[304,512]{1,0:T(8,128)(2,1)S(1)} collective-permute-done((bf16[304,512]{1,0:T(8,128)(2,1)S(1)}, bf16[304,512]{1,0:T(8,128)(2,1)S(1)}, u32[]{:S(2)}, u32[]{:S(2)}) %collective-permute-start.13) | collective-permute-done | bytes 311328 | tf_op jit(solution)/shard_map/ppermute | solution.py:649
  88.9 8.6 %collective-permute-done.15.seen_ref = bf16[288,1024]{1,0:T(8,128)(2,1)S(1)} collective-permute-done((bf16[288,1024]{1,0:T(8,128)(2,1)S(1)}, bf16[288,1024]{1,0:T(8,128)(2,1)S(1)}, u32[]{:S(2)}, u32[]{:S(2)}) %collective-permute-start.15) | collective-permute-done | bytes 589856 | tf_op jit(solution)/shard_map/ppermute | solution.py:649
  99.9 7.1 %collective-permute-done.16.seen_ref = bf16[288,768]{1,0:T(8,128)(2,1)S(1)} collective-permute-done((bf16[288,768]{1,0:T(8,128)(2,1)S(1)}, bf16[288,768]{1,0:T(8,128)(2,1)S(1)}, u32[]{:S(2)}, u32[]{:S(2)}) %collective-permute-start.16) | collective-permute-done | bytes 442400 | tf_op jit(solution)/shard_map/ppermute | solution.py:649
  108.8 4.5 %collective-permute-done.20.rest_1_ = bf16[288,512]{1,0:T(8,128)(2,1)S(1)} collective-permute-done((bf16[288,512]{1,0:T(8,128)(2,1)S(1)}, bf16[288,512]{1,0:T(8,128)(2,1)S(1)}, u32[]{:S(2)}, u32[]{:S(2)}) %collective-permute-start.20) | collective-permute-done | bytes 294944 | tf_op jit(solution)/shard_map/ppermute | solution.py:668
  113.8 2.6 %collective-permute-done.17.rest_1_ = bf16[288,256]{1,0:T(8,128)(2,1)S(1)} collective-permute-done((bf16[288,256]{1,0:T(8,128)(2,1)S(1)}, bf16[288,256]{1,0:T(8,128)(2,1)S(1)}, u32[]{:S(2)}, u32[]{:S(2)}) %collective-permute-start.17) | collective-permute-done | bytes 147488 | tf_op jit(solution)/shard_map/ppermute | solution.py:668
  116.9 3.7 %collective-permute-done.23.rest_1_ = bf16[288,384]{1,0:T(8,128)(2,1)S(1)} collective-permute-done((bf16[288,384]{1,0:T(8,128)(2,1)S(1)}, bf16[288,384]{1,0:T(8,128)(2,1)S(1)}, u32[]{:S(2)}, u32[]{:S(2)}) %collective-permute-start.23) | collective-permute-done | bytes 221216 | tf_op jit(solution)/shard_map/ppermute | solution.py:668
  127.0 2.6 %collective-permute-start.28 = (bf16[36,1536]{1,0:T(8,128)(2,1)S(1)}, bf16[36,1536]{1,0:T(8,128)(2,1)S(1)}, u32[]{:S(2)}, u32[]{:S(2)}) collective-permute-start(bf16[36,1536]{1,0:T(8,128)(2,1)S(1)} %get-tuple-element.144), channel_id=1, source_target_pairs={{0,12},{4,8},{8,4},{12,0},{16,28},{20,24},{24,20},{28,16},{1,13},{... | collective-permute-start | bytes 331784 | tf_op jit(solution)/shard_map/ppermute | solution.py:589
  136.2 5.7 %psum.7.stats_ref = f32[16,128]{1,0:T(8,128)S(1)} all-reduce(f32[16,128]{1,0:T(8,128)S(1)} %get-tuple-element.139), channel_id=1, replica_groups=mesh['seq'=8,'head'=4] {'head'}, use_global_device_ids=true, to_apply=%region_0.1 | all-reduce | flops 2048 | bytes 16384 | tf_op jit(solution)/shard_map/psum | solution.py:698
  142.8 4.8 %collective-permute-done.30.rest_5_ = bf16[36,1536]{1,0:T(8,128)(2,1)S(1)} collective-permute-done((bf16[36,1536]{1,0:T(8,128)(2,1)S(1)}, bf16[36,1536]{1,0:T(8,128)(2,1)S(1)}, u32[]{:S(2)}, u32[]{:S(2)}) %collective-permute-start.30) | collective-permute-done | bytes 110624 | tf_op jit(solution)/shard_map/ppermute | solution.py:589
  147.6 3.6 %collective-permute-done.31.rest_6_ = bf16[36,1536]{1,0:T(8,128)(2,1)S(1)} collective-permute-done((bf16[36,1536]{1,0:T(8,128)(2,1)S(1)}, bf16[36,1536]{1,0:T(8,128)(2,1)S(1)}, u32[]{:S(2)}, u32[]{:S(2)}) %collective-permute-start.31) | collective-permute-done | bytes 110624 | tf_op jit(solution)/shard_map/ppermute | solution.py:589
  153.5 2.5 %shard_map.148 = bf16[128,1536]{1,0:T(8,128)(2,1)} custom-call(bf16[8,36,128]{2,1,0:T(8,128)(2,1)S(1)} %get-tuple-element.140.high_ref, bf16[8,36,128]{2,1,0:T(8,128)(2,1)S(1)} %get-tuple-element.141.low_ref, bf16[128,1536]{1,0:T(8,128)(2,1)S(1)} %get-tuple-element.88.hidden_ref, bf16[36,1536]{1,0:T(8,128)(2,1)S(1)} %get-tuple-element.138.rest_0_, ...), custom_call_target="tpu_custom_call" | custom-call | flops 226492416 | bytes 1572864 | tf_op jit(solution)/shard_map/pallas_call | solution.py:708
  (87 shorter events, 49.9 us)
Async XLA Ops:
  9.4 7.8 %collective-permute-start.1 = (bf16[784,128]{1,0:T(8,128)(2,1)S(1)}, bf16[784,128]{1,0:T(8,128)(2,1)S(1)}, u32[]{:S(2)}, u32[]{:S(2)}) collective-permute-start(bf16[784,128]{1,0:T(8,128)(2,1)S(1)} %maximum_maximum_fusion), channel_id=1, source_target_pairs={{0,8},{4,12},{8,16},{12,20},{16,24},{20,28},{1,9},{5,13},{9,17},{1... | collective-permute-start | bytes 602120 | tf_op jit(solution)/shard_map/ppermute | solution.py:569
  17.5 11.2 %collective-permute-start.2 = (bf16[784,128]{1,0:T(8,128)(2,1)S(1)}, bf16[784,128]{1,0:T(8,128)(2,1)S(1)}, u32[]{:S(2)}, u32[]{:S(2)}) collective-permute-start(bf16[784,128]{1,0:T(8,128)(2,1)S(1)} %maximum_maximum_fusion.1), channel_id=1, source_target_pairs={{0,16},{4,20},{8,24},{12,28},{1,17},{5,21},{9,25},{13,29},{2,18},{... | collective-permute-start | bytes 602120 | tf_op jit(solution)/shard_map/ppermute | solution.py:569
  37.6 7.9 %collective-permute-start.4 = (bf16[36,1536]{1,0:T(8,128)(2,1)S(1)}, bf16[36,1536]{1,0:T(8,128)(2,1)S(1)}, u32[]{:S(2)}, u32[]{:S(2)}) collective-permute-start(bf16[36,1536]{1,0:T(8,128)(2,1)S(1)} %get-tuple-element.95), channel_id=1, source_target_pairs={{0,4},{4,0},{8,12},{12,8},{16,20},{20,16},{24,28},{28,24},{1,5},{5... | collective-permute-start | bytes 331784 | tf_op jit(solution)/shard_map/ppermute | solution.py:589
  39.1 7.8 %collective-permute-start.5 = (bf16[36,1536]{1,0:T(8,128)(2,1)S(1)}, bf16[36,1536]{1,0:T(8,128)(2,1)S(1)}, u32[]{:S(2)}, u32[]{:S(2)}) collective-permute-start(bf16[36,1536]{1,0:T(8,128)(2,1)S(1)} %get-tuple-element.96), channel_id=1, source_target_pairs={{0,8},{4,12},{8,0},{12,4},{16,24},{20,28},{24,16},{28,20},{1,9},{5... | collective-permute-start | bytes 331784 | tf_op jit(solution)/shard_map/ppermute | solution.py:589
  39.1 17.6 %collective-permute-start.6 = (bf16[36,1536]{1,0:T(8,128)(2,1)S(1)}, bf16[36,1536]{1,0:T(8,128)(2,1)S(1)}, u32[]{:S(2)}, u32[]{:S(2)}) collective-permute-start(bf16[36,1536]{1,0:T(8,128)(2,1)S(1)} %get-tuple-element.97), channel_id=1, source_target_pairs={{0,12},{4,8},{8,4},{12,0},{16,28},{20,24},{24,20},{28,16},{1,13},{... | collective-permute-start | bytes 331784 | tf_op jit(solution)/shard_map/ppermute | solution.py:589
  41.1 15.8 %collective-permute-start.7 = (bf16[36,1536]{1,0:T(8,128)(2,1)S(1)}, bf16[36,1536]{1,0:T(8,128)(2,1)S(1)}, u32[]{:S(2)}, u32[]{:S(2)}) collective-permute-start(bf16[36,1536]{1,0:T(8,128)(2,1)S(1)} %get-tuple-element.98), channel_id=1, source_target_pairs={{0,16},{4,20},{8,24},{12,28},{16,0},{20,4},{24,8},{28,12},{1,17},{... | collective-permute-start | bytes 331784 | tf_op jit(solution)/shard_map/ppermute | solution.py:589
  44.5 15.1 %collective-permute-start.8 = (bf16[36,1536]{1,0:T(8,128)(2,1)S(1)}, bf16[36,1536]{1,0:T(8,128)(2,1)S(1)}, u32[]{:S(2)}, u32[]{:S(2)}) collective-permute-start(bf16[36,1536]{1,0:T(8,128)(2,1)S(1)} %get-tuple-element.99), channel_id=1, source_target_pairs={{0,20},{4,16},{8,28},{12,24},{16,4},{20,0},{24,12},{28,8},{1,21},{... | collective-permute-start | bytes 331784 | tf_op jit(solution)/shard_map/ppermute | solution.py:589
  45.4 17.3 %collective-permute-start.9 = (bf16[36,1536]{1,0:T(8,128)(2,1)S(1)}, bf16[36,1536]{1,0:T(8,128)(2,1)S(1)}, u32[]{:S(2)}, u32[]{:S(2)}) collective-permute-start(bf16[36,1536]{1,0:T(8,128)(2,1)S(1)} %get-tuple-element.100), channel_id=1, source_target_pairs={{0,24},{4,28},{8,16},{12,20},{16,8},{20,12},{24,0},{28,4},{1,25},{... | collective-permute-start | bytes 331784 | tf_op jit(solution)/shard_map/ppermute | solution.py:589
  46.9 18.0 %collective-permute-start.10 = (bf16[36,1536]{1,0:T(8,128)(2,1)S(1)}, bf16[36,1536]{1,0:T(8,128)(2,1)S(1)}, u32[]{:S(2)}, u32[]{:S(2)}) collective-permute-start(bf16[36,1536]{1,0:T(8,128)(2,1)S(1)} %get-tuple-element.101), channel_id=1, source_target_pairs={{0,28},{4,24},{8,20},{12,16},{16,12},{20,8},{24,4},{28,0},{1,29},{... | collective-permute-start | bytes 331784 | tf_op jit(solution)/shard_map/ppermute | solution.py:589
  74.4 12.7 %collective-permute-start.14 = (bf16[288,1536]{1,0:T(8,128)(2,1)S(1)}, bf16[288,1536]{1,0:T(8,128)(2,1)S(1)}, u32[]{:S(2)}, u32[]{:S(2)}) collective-permute-start(bf16[288,1536]{1,0:T(8,128)(2,1)S(1)} %get-tuple-element.126), channel_id=1, source_target_pairs={{0,1},{1,0},{2,3},{3,2},{4,5},{5,4},{6,7},{7,6},{8,9},{9,8},{10,11... | collective-permute-start | bytes 2654216 | tf_op jit(solution)/shard_map/ppermute | solution.py:634
  74.5 10.3 %collective-permute-start.13 = (bf16[304,512]{1,0:T(8,128)(2,1)S(1)}, bf16[304,512]{1,0:T(8,128)(2,1)S(1)}, u32[]{:S(2)}, u32[]{:S(2)}) collective-permute-start(bf16[304,512]{1,0:T(8,128)(2,1)S(1)} %get-tuple-element.111), channel_id=1, source_target_pairs={{0,2},{1,3},{2,0},{3,1},{4,6},{5,7},{6,4},{7,5},{8,10},{9,11},{10,... | collective-permute-start | bytes 933896 | tf_op jit(solution)/shard_map/ppermute | solution.py:649
  76.3 21.2 %collective-permute-start.15 = (bf16[288,1024]{1,0:T(8,128)(2,1)S(1)}, bf16[288,1024]{1,0:T(8,128)(2,1)S(1)}, u32[]{:S(2)}, u32[]{:S(2)}) collective-permute-start(bf16[288,1024]{1,0:T(8,128)(2,1)S(1)} %get-tuple-element.117), channel_id=1, source_target_pairs={{0,2},{1,3},{2,0},{3,1},{4,6},{5,7},{6,4},{7,5},{8,10},{9,11},{10,... | collective-permute-start | bytes 1769480 | tf_op jit(solution)/shard_map/ppermute | solution.py:649
  87.3 19.6 %collective-permute-start.16 = (bf16[288,768]{1,0:T(8,128)(2,1)S(1)}, bf16[288,768]{1,0:T(8,128)(2,1)S(1)}, u32[]{:S(2)}, u32[]{:S(2)}) collective-permute-start(bf16[288,768]{1,0:T(8,128)(2,1)S(1)} %get-tuple-element.129), channel_id=1, source_target_pairs={{0,2},{1,3},{2,0},{3,1},{4,6},{5,7},{6,4},{7,5},{8,10},{9,11},{10,... | collective-permute-start | bytes 1327112 | tf_op jit(solution)/shard_map/ppermute | solution.py:649
  97.8 15.5 %collective-permute-start.20 = (bf16[288,512]{1,0:T(8,128)(2,1)S(1)}, bf16[288,512]{1,0:T(8,128)(2,1)S(1)}, u32[]{:S(2)}, u32[]{:S(2)}) collective-permute-start(bf16[288,512]{1,0:T(8,128)(2,1)S(1)} %shard_map.142.rest_0_), channel_id=1, source_target_pairs={{0,2},{1,3},{2,0},{3,1},{4,6},{5,7},{6,4},{7,5},{8,10},{9,11},{10,... | collective-permute-start | bytes 884744 | tf_op jit(solution)/shard_map/ppermute | solution.py:668
  99.3 17.1 %collective-permute-start.17 = (bf16[288,256]{1,0:T(8,128)(2,1)S(1)}, bf16[288,256]{1,0:T(8,128)(2,1)S(1)}, u32[]{:S(2)}, u32[]{:S(2)}) collective-permute-start(bf16[288,256]{1,0:T(8,128)(2,1)S(1)} %get-tuple-element.133.rest_0_), channel_id=1, source_target_pairs={{0,2},{1,3},{2,0},{3,1},{4,6},{5,7},{6,4},{7,5},{8,10},{9,11},{10,... | collective-permute-start | bytes 442376 | tf_op jit(solution)/shard_map/ppermute | solution.py:668
  107.2 13.4 %collective-permute-start.23 = (bf16[288,384]{1,0:T(8,128)(2,1)S(1)}, bf16[288,384]{1,0:T(8,128)(2,1)S(1)}, u32[]{:S(2)}, u32[]{:S(2)}) collective-permute-start(bf16[288,384]{1,0:T(8,128)(2,1)S(1)} %shard_map.143.rest_0_), channel_id=1, source_target_pairs={{0,2},{1,3},{2,0},{3,1},{4,6},{5,7},{6,4},{7,5},{8,10},{9,11},{10,... | collective-permute-start | bytes 663560 | tf_op jit(solution)/shard_map/ppermute | solution.py:668
  108.8 13.2 %collective-permute-start.21 = (bf16[288,512]{1,0:T(8,128)(2,1)S(1)}, bf16[288,512]{1,0:T(8,128)(2,1)S(1)}, u32[]{:S(2)}, u32[]{:S(2)}) collective-permute-start(bf16[288,512]{1,0:T(8,128)(2,1)S(1)} %shard_map.142.rest_0_), channel_id=1, source_target_pairs={{0,1},{1,0},{2,3},{3,2},{4,5},{5,4},{6,7},{7,6},{8,9},{9,8},{10,11... | collective-permute-start | bytes 884744 | tf_op jit(solution)/shard_map/ppermute | solution.py:669
  113.3 8.7 %collective-permute-start.22 = (bf16[288,512]{1,0:T(8,128)(2,1)S(1)}, bf16[288,512]{1,0:T(8,128)(2,1)S(1)}, u32[]{:S(2)}, u32[]{:S(2)}) collective-permute-start(bf16[288,512]{1,0:T(8,128)(2,1)S(1)} %collective-permute-done.20.rest_1_), channel_id=1, source_target_pairs={{0,1},{1,0},{2,3},{3,2},{4,5},{5,4},{6,7},{7,6},{8,9},{9,8},{10,11... | collective-permute-start | bytes 884744 | tf_op jit(solution)/shard_map/ppermute | solution.py:676
  116.4 7.5 %collective-permute-start.24 = (bf16[288,384]{1,0:T(8,128)(2,1)S(1)}, bf16[288,384]{1,0:T(8,128)(2,1)S(1)}, u32[]{:S(2)}, u32[]{:S(2)}) collective-permute-start(bf16[288,384]{1,0:T(8,128)(2,1)S(1)} %shard_map.143.rest_0_), channel_id=1, source_target_pairs={{0,1},{1,0},{2,3},{3,2},{4,5},{5,4},{6,7},{7,6},{8,9},{9,8},{10,11... | collective-permute-start | bytes 663560 | tf_op jit(solution)/shard_map/ppermute | solution.py:669
  127.0 15.8 %collective-permute-start.28 = (bf16[36,1536]{1,0:T(8,128)(2,1)S(1)}, bf16[36,1536]{1,0:T(8,128)(2,1)S(1)}, u32[]{:S(2)}, u32[]{:S(2)}) collective-permute-start(bf16[36,1536]{1,0:T(8,128)(2,1)S(1)} %get-tuple-element.144), channel_id=1, source_target_pairs={{0,12},{4,8},{8,4},{12,0},{16,28},{20,24},{24,20},{28,16},{1,13},{... | collective-permute-start | bytes 331784 | tf_op jit(solution)/shard_map/ppermute | solution.py:589
  129.6 13.3 %collective-permute-start.29 = (bf16[36,1536]{1,0:T(8,128)(2,1)S(1)}, bf16[36,1536]{1,0:T(8,128)(2,1)S(1)}, u32[]{:S(2)}, u32[]{:S(2)}) collective-permute-start(bf16[36,1536]{1,0:T(8,128)(2,1)S(1)} %get-tuple-element.145), channel_id=1, source_target_pairs={{0,16},{4,20},{8,24},{12,28},{16,0},{20,4},{24,8},{28,12},{1,17},{... | collective-permute-start | bytes 331784 | tf_op jit(solution)/shard_map/ppermute | solution.py:589
  130.7 16.9 %collective-permute-start.30 = (bf16[36,1536]{1,0:T(8,128)(2,1)S(1)}, bf16[36,1536]{1,0:T(8,128)(2,1)S(1)}, u32[]{:S(2)}, u32[]{:S(2)}) collective-permute-start(bf16[36,1536]{1,0:T(8,128)(2,1)S(1)} %get-tuple-element.146), channel_id=1, source_target_pairs={{0,20},{4,16},{8,28},{12,24},{16,4},{20,0},{24,12},{28,8},{1,21},{... | collective-permute-start | bytes 331784 | tf_op jit(solution)/shard_map/ppermute | solution.py:589
  132.8 18.4 %collective-permute-start.31 = (bf16[36,1536]{1,0:T(8,128)(2,1)S(1)}, bf16[36,1536]{1,0:T(8,128)(2,1)S(1)}, u32[]{:S(2)}, u32[]{:S(2)}) collective-permute-start(bf16[36,1536]{1,0:T(8,128)(2,1)S(1)} %get-tuple-element.147), channel_id=1, source_target_pairs={{0,24},{4,28},{8,16},{12,20},{16,8},{20,12},{24,0},{28,4},{1,25},{... | collective-permute-start | bytes 331784 | tf_op jit(solution)/shard_map/ppermute | solution.py:589
  134.2 19.3 %collective-permute-start.32 = (bf16[36,1536]{1,0:T(8,128)(2,1)S(1)}, bf16[36,1536]{1,0:T(8,128)(2,1)S(1)}, u32[]{:S(2)}, u32[]{:S(2)}) collective-permute-start(bf16[36,1536]{1,0:T(8,128)(2,1)S(1)} %get-tuple-element.148), channel_id=1, source_target_pairs={{0,28},{4,24},{8,20},{12,16},{16,12},{20,8},{24,4},{28,0},{1,29},{... | collective-permute-start | bytes 331784 | tf_op jit(solution)/shard_map/ppermute | solution.py:589
  (11 other events, 73.6 us)
